TPU v7x, 256 devices: a whole 4x4x8 slice. The times are simulated.
256 devices in a mesh: rep: 64 (over z, x, core), tp: 4 (over y).
Axes of the slice: x: 4, y: 4, z: 8, core: 2. Of those that a mesh axis runs over, the one named last changes fastest.
Arguments:
- suffix_source: bfloat16 [64, 384, 4096], P('rep', None, 'tp'), may hold values from -6 to 6
- suffix_accept: bfloat16 [64, 384, 4096], P('rep', None, 'tp'), may hold values from -3 to 3
- suffix_address: bfloat16 [64, 384, 4096], P('rep', None, 'tp'), may hold values from -3 to 3
- guess_lane_source: bfloat16 [128, 16, 4096], P('rep', None, 'tp'), may hold values from -6 to 6
- guess_lane_accept: bfloat16 [128, 16, 4096], P('rep', None, 'tp'), may hold values from -3 to 3
- guess_lane_address: bfloat16 [128, 16, 4096], P('rep', None, 'tp'), may hold values from -3 to 3
- content_map: bfloat16 [4096, 4096], P(None, 'tp'), may hold values from -0.09375 to 0.09375
- forget_shrink_map: bfloat16 [4096, 128], replicated, may hold values from -0.09375 to 0.09375
- forget_expand_map: bfloat16 [128, 4096], P(None, 'tp'), may hold values from -0.35351562 to 0.35351562
- forget_lane_anchor: float32 [4096], P('tp'), may hold values from -12 to -3
- present_boost: float32 [4096], P('tp'), may hold values from -1.5 to 1.5
- content_blend_share: float32 [4096], P('tp'), may hold values from 0 to 1
- forget_blend_share: float32 [4096], P('tp'), may hold values from 0 to 1
- lane_normal_scale: float32 [4096], P('tp'), may hold values from 0.5 to 1.5
- lane_normal_shift: float32 [4096], P('tp'), may hold values from -1.2 to 1.2
- kernel_memory_saved: float32 [128, 64, 4096], P(None, 'rep', 'tp'), may hold values from -6 to 6
- prior_source_saved: bfloat16 [128, 64, 64], P(None, 'rep', 'tp'), may hold values from -6 to 6
- lane_owner: int32 [128], replicated, may hold values from 0 to 127, as said below
- request_spans: int32 [128], replicated, may hold values from 16 to 400, as said below
- admitted_guesses: int32 [128], replicated, may hold values from 0 to 16
Outputs:
- tail_out: bfloat16 [64, 384, 4096], P('rep', None, 'tp')
- draft_out: bfloat16 [128, 16, 4096], P('rep', None, 'tp')
- state_out: float32 [128, 64, 4096], P(None, 'rep', 'tp')
- shift_out: bfloat16 [128, 64, 64], P(None, 'rep', 'tp')
Inputs may be any that keep to these rules, and one draw needn't show every extreme that they name: `lane_owner`: a permutation of the request numbers. `request_spans`: exactly 8 requests have 16 + 384 tokens and the others 16; a long request is always dealt to a slot s with s % 2 == 0; each aligned block of 8 consecutive groups holds exactly one group whose first slot is long; the tail buffers of groups whose first slot is not long are not read.
All inputs are finite; a program needn't handle non-finite values.
Results may differ from a plain program's by a relative error of at most 0.0051.
The roundings to bfloat16 on the way count: a program that leaves them out, or rounds other values in their place, can miss the bound.
Values may be sent and summed in bfloat16 or wider, within the bound.
A program may use at most 128 MiB of HBM per device.

v0:
```python
import jax
import jax.numpy as jnp
from jax import lax
from jax.sharding import PartitionSpec as P

SUBSPACE_SPAN = 64
DRAFT = 16


HIGH = lax.Precision.HIGHEST
EPS = 0.00064


def group_norm(answer_collection, lane_normal_scale, lane_normal_shift):
    center = answer_collection - jnp.mean(answer_collection, axis=-1, keepdims=True)
    spread = jnp.mean(center * center, axis=-1, keepdims=True)
    normed = (center / jnp.sqrt(spread + EPS)).reshape(answer_collection.shape[0], -1)
    return (normed * lane_normal_scale + lane_normal_shift).astype(jnp.bfloat16)


def token_mix(current, previous, mixing):
    present = current.astype(jnp.float32)
    return (present + (previous.astype(jnp.float32) - present) * mixing).astype(jnp.bfloat16)


def project(
    mixed_value,
    decay_mixed_input,
    content_map,
    forget_shrink_map,
    forget_expand_map,
    forget_lane_anchor,
):
    acc_value = jnp.dot(
        lax.all_gather(mixed_value, "tp", axis=1, tiled=True),
        content_map,
        preferred_element_type=jnp.float32,
    )
    decay_accumulated = jnp.dot(
        lax.all_gather(decay_mixed_input, "tp", axis=1, tiled=True),
        forget_shrink_map,
        preferred_element_type=jnp.float32,
    )
    acc_value, decay_accumulated = (acc_value, decay_accumulated)
    content_vectors = acc_value.astype(jnp.bfloat16)
    decay_low_rank = jnp.tanh(decay_accumulated).astype(jnp.bfloat16)
    forget_logscale = -jnp.exp(
        forget_lane_anchor
        + jnp.dot(decay_low_rank, forget_expand_map, preferred_element_type=jnp.float32)
    )
    return (content_vectors, forget_logscale)


def process_blocks(
    accept_vectors, address_vectors, content_vectors, forget_logscale, ongoing_memory, lanes_boost
):
    total_steps = accept_vectors.shape[0]
    block_len = min(64, total_steps)
    block_count = total_steps // block_len
    lower = jnp.arange(block_len)[:, None] > jnp.arange(block_len)[None, :]

    def shape_blocks(array):
        return array.reshape(block_count, block_len, array.shape[1], array.shape[2])

    def one_block(threaded_pair, source_vectors):
        accept_vectors_all, address_vectors_all, value_rows_batch, rate_b = source_vectors
        inclusive = jnp.cumsum(rate_b, axis=0)
        exclusive = inclusive - rate_b
        middle = inclusive[block_len // 2]
        recept_scaled = accept_vectors_all * jnp.exp(exclusive - middle)
        keys_scaled = address_vectors_all * jnp.exp(middle - inclusive)
        scores = jnp.einsum("thi,shi->hts", recept_scaled, keys_scaled, precision=HIGH)
        scores = jnp.where(lower[None], scores, 0.0)
        answer_vectors = jnp.einsum("hts,shj->thj", scores, value_rows_batch, precision=HIGH)
        answer_vectors = answer_vectors + jnp.einsum(
            "thi,hij->thj", accept_vectors_all * jnp.exp(exclusive), threaded_pair, precision=HIGH
        )
        answer_vectors = (
            answer_vectors
            + jnp.sum(
                accept_vectors_all * lanes_boost * address_vectors_all, axis=-1, keepdims=True
            )
            * value_rows_batch
        )
        total = inclusive[-1]
        threaded_pair = jnp.exp(total)[:, :, None] * threaded_pair + jnp.einsum(
            "shi,shj->hij",
            address_vectors_all * jnp.exp(total - inclusive),
            value_rows_batch,
            precision=HIGH,
        )
        return (threaded_pair, answer_vectors)

    closing_answer, answer_collection = lax.scan(
        one_block,
        ongoing_memory,
        (
            shape_blocks(accept_vectors),
            shape_blocks(address_vectors),
            shape_blocks(content_vectors),
            shape_blocks(forget_logscale),
        ),
    )
    return (
        answer_collection.reshape(total_steps, accept_vectors.shape[1], accept_vectors.shape[2]),
        closing_answer,
    )


def local(
    suffix_source,
    suffix_accept,
    suffix_address,
    guess_lane_source,
    guess_lane_accept,
    guess_lane_address,
    content_map,
    forget_shrink_map,
    forget_expand_map,
    forget_lane_anchor,
    present_boost,
    content_blend_share,
    forget_blend_share,
    lane_normal_scale,
    lane_normal_shift,
    kernel_memory_saved,
    prior_source_saved,
    lane_owner,
    request_spans,
    admitted_guesses,
):
    local_width = content_map.shape[1]
    lanes_owned = local_width // SUBSPACE_SPAN
    slots = guess_lane_source.shape[0]
    squad_index = lax.axis_index("rep")
    slot_ids = squad_index * slots + jnp.arange(slots, dtype=jnp.int32)
    my_reqs = lane_owner[slot_ids]
    slot_long = request_spans[my_reqs] > DRAFT
    group_long = slot_long[0]
    lanes_boost = present_boost.reshape(lanes_owned, SUBSPACE_SPAN)
    ordered_state = kernel_memory_saved[lane_owner]
    ordered_shift = prior_source_saved[lane_owner].astype(jnp.float32)
    got_state, got_shift = (
        lax.all_to_all(ordered_state, "rep", split_axis=0, concat_axis=1, tiled=True),
        lax.all_to_all(ordered_shift, "rep", split_axis=0, concat_axis=1, tiled=True),
    )
    start = got_state.reshape(slots, SUBSPACE_SPAN, lanes_owned, SUBSPACE_SPAN).transpose(
        0, 2, 1, 3
    )
    start_prev = got_shift.astype(jnp.bfloat16).transpose(0, 2, 1).reshape(slots, local_width)

    def divide_lanes(array):
        return array.astype(jnp.float32).reshape(array.shape[0], lanes_owned, SUBSPACE_SPAN)

    tail_tokens = suffix_source[0]
    tail_len = tail_tokens.shape[0]
    tail_prev = jnp.concatenate([start_prev[:1], tail_tokens[:-1]], axis=0)
    tail_value = token_mix(tail_tokens, tail_prev, content_blend_share)
    tail_decay = token_mix(tail_tokens, tail_prev, forget_blend_share)
    tail_recept = suffix_accept[0]
    tail_keys = suffix_address[0]
    first = jnp.where(slot_long[:, None], tail_tokens[-1][None, :], start_prev)
    draft_prev = jnp.concatenate([first[:, None], guess_lane_source[:, :-1]], axis=1)
    draft_value = token_mix(guess_lane_source, draft_prev, content_blend_share).reshape(
        slots * DRAFT, local_width
    )
    draft_decay = token_mix(guess_lane_source, draft_prev, forget_blend_share).reshape(
        slots * DRAFT, local_width
    )
    content_vectors, forget_logscale = project(
        jnp.concatenate([tail_value, draft_value], axis=0),
        jnp.concatenate([tail_decay, draft_decay], axis=0),
        content_map,
        forget_shrink_map,
        forget_expand_map,
        forget_lane_anchor,
    )
    tail_y, tail_end = process_blocks(
        divide_lanes(tail_recept),
        divide_lanes(tail_keys),
        divide_lanes(content_vectors[:tail_len]),
        forget_logscale[:tail_len].reshape(tail_len, lanes_owned, SUBSPACE_SPAN),
        start[0],
        lanes_boost,
    )
    tail_norm = group_norm(tail_y, lane_normal_scale, lane_normal_shift)
    tail_out = jnp.where(group_long, tail_norm, jnp.zeros_like(tail_norm))[None]
    guess_content = (
        content_vectors[tail_len:]
        .astype(jnp.float32)
        .reshape(slots, DRAFT, lanes_owned, SUBSPACE_SPAN)
    )
    guess_forget = forget_logscale[tail_len:].reshape(slots, DRAFT, lanes_owned, SUBSPACE_SPAN)
    guess_accept = guess_lane_accept.astype(jnp.float32).reshape(
        slots, DRAFT, lanes_owned, SUBSPACE_SPAN
    )
    guess_address = guess_lane_address.astype(jnp.float32).reshape(
        slots, DRAFT, lanes_owned, SUBSPACE_SPAN
    )
    trailing_pair = jnp.where(slot_long[:, None, None, None], tail_end[None], start)
    draft_y, draft_final = jax.vmap(process_blocks, in_axes=(0, 0, 0, 0, 0, None))(
        guess_accept, guess_address, guess_content, guess_forget, trailing_pair, lanes_boost
    )
    draft_out = group_norm(
        draft_y.reshape(slots * DRAFT, lanes_owned, SUBSPACE_SPAN),
        lane_normal_scale,
        lane_normal_shift,
    ).reshape(slots, DRAFT, local_width)
    count = admitted_guesses[my_reqs]
    taken = jnp.arange(DRAFT, dtype=jnp.int32)[None, :] < count[:, None]
    inclusive_d = jnp.cumsum(guess_forget, axis=1)
    upto = jnp.sum(jnp.where(taken[:, :, None, None], guess_forget, 0.0), axis=1)
    weight = jnp.where(taken[:, :, None, None], jnp.exp(upto[:, None] - inclusive_d), 0.0)
    chosen = jnp.exp(upto)[..., None] * trailing_pair + jnp.einsum(
        "sthi,sthj->shij", guess_address * weight, guess_content, precision=HIGH
    )
    edge_row = guess_lane_source[jnp.arange(slots), jnp.maximum(count - 1, 0)]
    edge = jnp.where((count > 0)[:, None], edge_row, first)
    ret_state = chosen.transpose(0, 2, 1, 3).reshape(slots, SUBSPACE_SPAN, local_width)
    ret_shift = (
        edge.reshape(slots, lanes_owned, SUBSPACE_SPAN).transpose(0, 2, 1).astype(jnp.float32)
    )
    back_state, back_shift = (
        lax.all_to_all(ret_state, "rep", split_axis=1, concat_axis=0, tiled=True),
        lax.all_to_all(ret_shift, "rep", split_axis=1, concat_axis=0, tiled=True),
    )
    total_reqs = lane_owner.shape[0]
    inverse = (
        jnp.zeros((total_reqs,), jnp.int32)
        .at[lane_owner]
        .set(jnp.arange(total_reqs, dtype=jnp.int32))
    )
    state_out = back_state[inverse]
    shift_out = back_shift[inverse].astype(jnp.bfloat16)
    return (tail_out, draft_out, state_out, shift_out)


def solution(mesh):
    placed = (
        P("rep", None, "tp"),
        P("rep", None, "tp"),
        P("rep", None, "tp"),
        P("rep", None, "tp"),
        P("rep", None, "tp"),
        P("rep", None, "tp"),
        P(None, "tp"),
        P(),
        P(None, "tp"),
        P("tp"),
        P("tp"),
        P("tp"),
        P("tp"),
        P("tp"),
        P("tp"),
        P(None, "rep", "tp"),
        P(None, "rep", "tp"),
        P(),
        P(),
        P(),
    )
    return jax.shard_map(
        local,
        mesh=mesh,
        in_specs=placed,
        out_specs=(
            P("rep", None, "tp"),
            P("rep", None, "tp"),
            P(None, "rep", "tp"),
            P(None, "rep", "tp"),
        ),
        check_vma=False,
    )
```

profile of v0, /device:TPU:1, one launch (start us, length us, event | category | flops | bytes accessed | tf_op | source)
XLA Modules:
  0.0 245.0 jit_solution(6929239159110475393)
XLA Ops:
  10.2 13.0 %all-to-all-start.1 = ((bf16[128,1,16]{2,1,0:T(2,128)(2,1)}), bf16[128,1,16]{2,1,0:T(2,128)(2,1)S(1)}, u32[]{:S(2)}, u32[]{:S(2)}) async-start(bf16[128,1,16]{2,1,0:T(2,128)(2,1)} %convert.36), calls=%async_computation.1 | async-start | bytes 131072 | tf_op jit(solution)/shard_map/all_to_all | solution.py:145
  23.3 1.3 gather_fusion
  26.0 7.3 %all-to-all-done.1 = bf16[128,1,16]{2,1,0:T(2,128)(2,1)S(1)} async-done(((bf16[128,1,16]{2,1,0:T(2,128)(2,1)}), bf16[128,1,16]{2,1,0:T(2,128)(2,1)S(1)}, u32[]{:S(2)}, u32[]{:S(2)}) %all-to-all-start.1) | async-done | bytes 4128 | tf_op jit(solution)/shard_map/all_to_all | solution.py:145
  39.5 4.4 %all-to-all-start.3 = ((bf16[2,64,16]{2,0,1:T(2,128)(2,1)}), bf16[2,64,16]{2,0,1:T(2,128)(2,1)S(1)}, u32[]{:S(2)}, u32[]{:S(2)}) async-start(bf16[2,64,16]{2,0,1:T(2,128)(2,1)} %convert_bitcast_fusion), calls=%async_computation.3 | async-start | bytes 65536 | tf_op jit(solution)/shard_map/all_to_all | solution.py:225
  44.9 1.3 copy.156
  46.2 7.1 %all-to-all-done.3 = bf16[2,64,16]{2,0,1:T(2,128)(2,1)S(1)} async-done(((bf16[2,64,16]{2,0,1:T(2,128)(2,1)}), bf16[2,64,16]{2,0,1:T(2,128)(2,1)S(1)}, u32[]{:S(2)}, u32[]{:S(2)}) %all-to-all-start.3) | async-done | bytes 4128 | tf_op jit(solution)/shard_map/all_to_all | solution.py:225
  53.3 4.7 %all-to-all-start = ((f32[128,1,1024]{2,1,0:T(1,128)}), f32[128,1,1024]{2,1,0:T(1,128)S(1)}, u32[]{:S(2)}, u32[]{:S(2)}) async-start(f32[128,1,1024]{2,1,0:T(1,128)} %copy.156), calls=%async_computation | async-start | bytes 1048576 | tf_op jit(solution)/shard_map/all_to_all | solution.py:144
  61.0 2.2 reshape.402
  63.2 3.4 %reshape.400 = f32[6,64,16,64]{3,2,1,0:T(8,128)} reshape(bf16[1,384,1024]{2,1,0:T(8,128)(2,1)} %param.24) | data formatting | bytes 2359296 | tf_op jit(solution)/shard_map/convert_element_type | solution.py:153
  69.2 6.7 %all-to-all-done = f32[128,1,1024]{2,1,0:T(1,128)S(1)} async-done(((f32[128,1,1024]{2,1,0:T(1,128)}), f32[128,1,1024]{2,1,0:T(1,128)S(1)}, u32[]{:S(2)}, u32[]{:S(2)}) %all-to-all-start) | async-done | bytes 524320 | tf_op jit(solution)/shard_map/all_to_all | solution.py:144
  77.6 8.1 %convolution_convert_fusion = bf16[416,1024]{1,0:T(8,128)(2,1)S(1)} fusion(bf16[416,4096]{1,0:T(8,128)(2,1)} %all-gather.5.cloned.1.call-done, bf16[4096,1024]{1,0:T(8,128)(2,1)} %param.28), kind=kOutput, calls=%fused_computation.48 | convolution fusion | flops 3490086912 | bytes 12648448 | tf_op jit(solution)/shard_map/dot_general | solution.py:34
  86.3 1.4 slice_convert_fusion
  87.7 33.6 %all-gather.3.cloned.1.call-done = bf16[416,4096]{1,0:T(8,128)(2,1)} async-done(((bf16[416,1024]{1,0:T(8,128)(2,1)}), bf16[416,4096]{1,0:T(8,128)(2,1)}) %all-gather.3.cloned.1.call-update) | async-done | bytes 3407888 | tf_op jit(solution)/shard_map/all_gather | solution.py:40
  121.3 3.7 %exponential_negate_fusion = f32[416,1024]{1,0:T(8,128)S(1)} fusion(bf16[128,1024]{1,0:T(8,128)(2,1)S(1)} %copy-done.18, bf16[416,4096]{1,0:T(8,128)(2,1)} %all-gather.3.cloned.1.call-done, bf16[4096,128]{1,0:T(8,128)(2,1)S(1)} %copy-done, f32[1024]{0:T(1024)} %param.31), kind=kOutput, calls=%fused_computation.44 | convolution fusion | flops 546164736 | bytes 6426624 | tf_op jit(solution)/shard_map/dot_general | solution.py:49
  126.4 1.4 fusion.41
  129.2 2.2 reshape_reshape.7
  131.4 3.4 %reshape.401 = f32[6,64,16,64]{3,2,1,0:T(8,128)} reshape(f32[384,1024]{1,0:T(8,128)} %slice_convert_fusion) | data formatting | bytes 3145728 | tf_op jit(solution)/shard_map/reshape;reshape | solution.py:63
  134.8 60.3 %while.3 = (s32[]{:T(128)}, f32[16,64,64]{2,1,0:T(8,128)S(1)}, f32[6,64,16,64]{3,1,2,0:T(8,128)}, f32[6,64,16,64]{3,2,1,0:T(8,128)}, f32[6,64,16,64]{3,2,1,0:T(8...) while((s32[]{:T(128)}, f32[16,64,64]{2,1,0:T(8,128)S(1)}, ...), condition=%wide.region_3.4_spmd.clone, body=%wide.region_0.3_spmd.clone.sunk | while | flops 206572544 | bytes 8724625 | solution.py:94
  137.1 2.5 %bitcast_multiply_fusion.6 = (f32[64,16,64]{2,1,0:T(8,128)S(1)}, f32[64,16,64]{2,1,0:T(8,128)S(1)}, f32[64,16]{1,0:T(8,128)S(1)}, f32[64,16,64]{2,1,0:T(8,128)S(1)}, f32[64,16,64]{2,1,0:T(8,128)}) fusion(f32[64,16,64]{2,1,0:T(8,128)S(1)} %fusion.68, f32[6,64,16,64]{3,2,1,0:T(8,128)} %get-tuple-element.282, s32[]{:T(128)S(6)} %copy.261, ...), kind=kLoop, calls=%fused_computation.24.clone.1 | loop fusion | flops 719872 | bytes 2113540 | tf_op jit(solution)/shard_map/while/body/eval_jaxpr/mul | solution.py:71
  141.7 1.8 fusion.70
  143.5 1.3 convolution_add_fusion.3
  147.1 2.5 %bitcast_multiply_fusion.6 = (f32[64,16,64]{2,1,0:T(8,128)S(1)}, f32[64,16,64]{2,1,0:T(8,128)S(1)}, f32[64,16]{1,0:T(8,128)S(1)}, f32[64,16,64]{2,1,0:T(8,128)S(1)}, f32[64,16,64]{2,1,0:T(8,128)}) fusion(f32[64,16,64]{2,1,0:T(8,128)S(1)} %fusion.68, f32[6,64,16,64]{3,2,1,0:T(8,128)} %get-tuple-element.282, s32[]{:T(128)S(6)} %copy.261, ...), kind=kLoop, calls=%fused_computation.24.clone.1 | loop fusion | flops 719872 | bytes 2113540 | tf_op jit(solution)/shard_map/while/body/eval_jaxpr/mul | solution.py:71
  151.8 1.8 fusion.70
  153.6 1.3 convolution_add_fusion.3
  157.2 2.5 %bitcast_multiply_fusion.6 = (f32[64,16,64]{2,1,0:T(8,128)S(1)}, f32[64,16,64]{2,1,0:T(8,128)S(1)}, f32[64,16]{1,0:T(8,128)S(1)}, f32[64,16,64]{2,1,0:T(8,128)S(1)}, f32[64,16,64]{2,1,0:T(8,128)}) fusion(f32[64,16,64]{2,1,0:T(8,128)S(1)} %fusion.68, f32[6,64,16,64]{3,2,1,0:T(8,128)} %get-tuple-element.282, s32[]{:T(128)S(6)} %copy.261, ...), kind=kLoop, calls=%fused_computation.24.clone.1 | loop fusion | flops 719872 | bytes 2113540 | tf_op jit(solution)/shard_map/while/body/eval_jaxpr/mul | solution.py:71
  161.8 1.8 fusion.70
  163.6 1.3 convolution_add_fusion.3
  167.2 2.5 %bitcast_multiply_fusion.6 = (f32[64,16,64]{2,1,0:T(8,128)S(1)}, f32[64,16,64]{2,1,0:T(8,128)S(1)}, f32[64,16]{1,0:T(8,128)S(1)}, f32[64,16,64]{2,1,0:T(8,128)S(1)}, f32[64,16,64]{2,1,0:T(8,128)}) fusion(f32[64,16,64]{2,1,0:T(8,128)S(1)} %fusion.68, f32[6,64,16,64]{3,2,1,0:T(8,128)} %get-tuple-element.282, s32[]{:T(128)S(6)} %copy.261, ...), kind=kLoop, calls=%fused_computation.24.clone.1 | loop fusion | flops 719872 | bytes 2113540 | tf_op jit(solution)/shard_map/while/body/eval_jaxpr/mul | solution.py:71
  171.9 1.8 fusion.70
  173.7 1.3 convolution_add_fusion.3
  177.3 2.5 %bitcast_multiply_fusion.6 = (f32[64,16,64]{2,1,0:T(8,128)S(1)}, f32[64,16,64]{2,1,0:T(8,128)S(1)}, f32[64,16]{1,0:T(8,128)S(1)}, f32[64,16,64]{2,1,0:T(8,128)S(1)}, f32[64,16,64]{2,1,0:T(8,128)}) fusion(f32[64,16,64]{2,1,0:T(8,128)S(1)} %fusion.68, f32[6,64,16,64]{3,2,1,0:T(8,128)} %get-tuple-element.282, s32[]{:T(128)S(6)} %copy.261, ...), kind=kLoop, calls=%fused_computation.24.clone.1 | loop fusion | flops 719872 | bytes 2113540 | tf_op jit(solution)/shard_map/while/body/eval_jaxpr/mul | solution.py:71
  182.0 1.8 fusion.70
  183.7 1.3 convolution_add_fusion.3
  187.3 2.5 %bitcast_multiply_fusion.6 = (f32[64,16,64]{2,1,0:T(8,128)S(1)}, f32[64,16,64]{2,1,0:T(8,128)S(1)}, f32[64,16]{1,0:T(8,128)S(1)}, f32[64,16,64]{2,1,0:T(8,128)S(1)}, f32[64,16,64]{2,1,0:T(8,128)}) fusion(f32[64,16,64]{2,1,0:T(8,128)S(1)} %fusion.68, f32[6,64,16,64]{3,2,1,0:T(8,128)} %get-tuple-element.282, s32[]{:T(128)S(6)} %copy.261, ...), kind=kLoop, calls=%fused_computation.24.clone.1 | loop fusion | flops 719872 | bytes 2113540 | tf_op jit(solution)/shard_map/while/body/eval_jaxpr/mul | solution.py:71
  192.0 1.8 fusion.70
  193.8 1.3 convolution_add_fusion.3
  195.1 2.8 %reduce_sum.64 = f32[6,64,16]{1,2,0:T(8,128)S(1)} reduce(f32[6,64,16,64]{3,1,2,0:T(8,128)} %get-tuple-element.79, f32[]{:T(128)} %constant.69.clone.1), dimensions={3}, to_apply=%region_4.5 | reduce | flops 387072 | bytes 1597444 | tf_op jit(solution)/shard_map/reduce_sum | solution.py:15
  197.9 3.3 %multiply_reduce_fusion = f32[6,64,16]{1,2,0:T(8,128)S(1)} fusion(f32[6,64,16,64]{3,1,2,0:T(8,128)} %get-tuple-element.79, f32[6,64,16]{1,2,0:T(8,128)S(1)} %broadcast_multiply_fusion), kind=kLoop, calls=%fused_computation.40 | loop fusion | flops 1173504 | bytes 1622016 | tf_op jit(solution)/shard_map/reduce_sum | solution.py:16
  202.2 1.4 fusion.19
  204.2 1.3 reshape.497
  205.5 10.8 %all-to-all-start.2 = ((f32[2,64,1024]{2,0,1:T(2,128)}), f32[2,64,1024]{2,0,1:T(2,128)S(1)}, u32[]{:S(2)}, u32[]{:S(2)}) async-start(f32[2,64,1024]{2,0,1:T(2,128)} %reshape.497), calls=%async_computation.2 | async-start | bytes 1048576 | tf_op jit(solution)/shard_map/all_to_all | solution.py:224
  216.4 1.3 fusion.24
  218.9 3.5 %copy.165 = f32[6,64,16,64]{3,2,1,0:T(8,128)} copy(f32[6,64,16,64]{3,1,2,0:T(8,128)S(1)} %copy-done.4) | data formatting | bytes 3145728 | tf_op jit(solution)/shard_map/while | solution.py:94
  222.3 3.7 %reshape.397 = f32[1,384,1024]{2,1,0:T(8,128)} reshape(f32[6,64,16,64]{3,2,1,0:T(8,128)} %copy.165) | data formatting | bytes 3145728 | tf_op jit(solution)/shard_map/reshape | solution.py:105
  227.5 1.6 copy.167
  229.2 1.6 copy.169
  231.5 3.9 %fusion.26 = bf16[1,384,1024]{2,1,0:T(8,128)(2,1)} fusion(f32[1024]{0:T(1024)S(1)} %copy-done.26, f32[1024]{0:T(1024)S(1)} %copy-done.27, f32[1,384,1024]{2,1,0:T(8,128)} %copy.169, f32[1,384,1024]{2,1,0:T(8,128)} %reshape.397, f32[1,384,1024]{2,1,0:T(8,128)} %copy.167, pred[]{:T(512)S(1)} %bitcast.201), kind=kLoop, calls=%fused_computation.66 | loop fusion | flops 2359296 | bytes 5513217 | tf_op jit(solution)/shard_map/jit(_where)/select_n | solution.py:187
  236.8 1.3 copy.190
  (222 shorter events, 54.7 us)
Async XLA Ops:
  7.2 114.1 %copy-start = (bf16[4096,128]{1,0:T(8,128)(2,1)S(1)}, bf16[4096,128]{1,0:T(8,128)(2,1)}, u32[]{:S(2)}) copy-start(bf16[4096,128]{1,0:T(8,128)(2,1)} %param.29) | copy-start | bytes 3145732
  7.2 18.7 %copy-start.8 = (bf16[1,384,1024]{2,1,0:T(8,128)(2,1)S(1)}, bf16[1,384,1024]{2,1,0:T(8,128)(2,1)}, u32[]{:S(2)}) copy-start(bf16[1,384,1024]{2,1,0:T(8,128)(2,1)} %param.22) | copy-start | bytes 2359300
  8.8 25.0 %copy-start.17 = (bf16[2,16,1024]{2,1,0:T(8,128)(2,1)S(1)}, bf16[2,16,1024]{2,1,0:T(8,128)(2,1)}, u32[]{:S(2)}) copy-start(bf16[2,16,1024]{2,1,0:T(8,128)(2,1)} %param.25) | copy-start | bytes 196612
  8.8 25.0 %copy-start.24 = (f32[1024]{0:T(1024)S(1)}, f32[1024]{0:T(1024)}, u32[]{:S(2)}) copy-start(f32[1024]{0:T(1024)} %param.33) | copy-start | bytes 12292
  8.8 25.0 %copy-start.25 = (f32[1024]{0:T(1024)S(1)}, f32[1024]{0:T(1024)}, u32[]{:S(2)}) copy-start(f32[1024]{0:T(1024)} %param.34) | copy-start | bytes 12292
  10.2 23.1 %all-to-all-start.1 = ((bf16[128,1,16]{2,1,0:T(2,128)(2,1)}), bf16[128,1,16]{2,1,0:T(2,128)(2,1)S(1)}, u32[]{:S(2)}, u32[]{:S(2)}) async-start(bf16[128,1,16]{2,1,0:T(2,128)(2,1)} %convert.36), calls=%async_computation.1 | async-start | bytes 131072 | tf_op jit(solution)/shard_map/all_to_all | solution.py:145
  23.2 54.4 %all-gather.5.cloned.1.call-start = ((), (), s32[]{:S(2)}) async-start(), calls=%async_computation.5 | async-start | bytes 4259840 | tf_op jit(solution)/shard_map/all_gather | solution.py:35
  35.0 1.1 copy-start.20
  36.0 1.2 copy-start.2
  36.0 7.9 %copy-start.16 = (f32[128,1,1024]{2,1,0:T(1,128)S(1)}, f32[128,1,1024]{2,1,0:T(1,128)}, u32[]{:S(2)}) copy-start(f32[128,1,1024]{2,1,0:T(1,128)} %param.37) | copy-start | bytes 1572868
  36.0 85.2 %all-gather.3.cloned.1.call-start = ((), (), s32[]{:S(2)}) async-start(), calls=%async_computation.4 | async-start | bytes 4259840 | tf_op jit(solution)/shard_map/all_gather | solution.py:40
  39.5 13.8 %all-to-all-start.3 = ((bf16[2,64,16]{2,0,1:T(2,128)(2,1)}), bf16[2,64,16]{2,0,1:T(2,128)(2,1)S(1)}, u32[]{:S(2)}, u32[]{:S(2)}) async-start(bf16[2,64,16]{2,0,1:T(2,128)(2,1)} %convert_bitcast_fusion), calls=%async_computation.3 | async-start | bytes 65536 | tf_op jit(solution)/shard_map/all_to_all | solution.py:225
  44.8 14.4 %copy-start.21 = (f32[1024]{0:T(1024)S(1)}, f32[1024]{0:T(1024)}, u32[]{:S(2)}) copy-start(f32[1024]{0:T(1024)} %param.32) | copy-start | bytes 12292
  44.8 14.5 %copy-start.22 = (bf16[2,16,1024]{2,1,0:T(8,128)(2,1)S(1)}, bf16[2,16,1024]{2,1,0:T(8,128)(2,1)}, u32[]{:S(2)}) copy-start(bf16[2,16,1024]{2,1,0:T(8,128)(2,1)} %param.26) | copy-start | bytes 196612
  44.8 15.3 %copy-start.23 = (bf16[2,16,1024]{2,1,0:T(8,128)(2,1)S(1)}, bf16[2,16,1024]{2,1,0:T(8,128)(2,1)}, u32[]{:S(2)}) copy-start(bf16[2,16,1024]{2,1,0:T(8,128)(2,1)} %param.27) | copy-start | bytes 196612
  44.9 16.2 %copy-start.15 = (bf16[1,384,1024]{2,1,0:T(8,128)(2,1)S(1)}, bf16[1,384,1024]{2,1,0:T(8,128)(2,1)}, u32[]{:S(2)}) copy-start(bf16[1,384,1024]{2,1,0:T(8,128)(2,1)} %param.23) | copy-start | bytes 2359300
  53.3 22.6 %all-to-all-start = ((f32[128,1,1024]{2,1,0:T(1,128)}), f32[128,1,1024]{2,1,0:T(1,128)S(1)}, u32[]{:S(2)}, u32[]{:S(2)}) async-start(f32[128,1,1024]{2,1,0:T(1,128)} %copy.156), calls=%async_computation | async-start | bytes 1048576 | tf_op jit(solution)/shard_map/all_to_all | solution.py:144
  67.2 8.9 %copy-start.29 = (s32[1024]{0:T(1024)}, s32[1024]{0:T(1024)S(1)}, u32[]{:S(2)}) copy-start(s32[1024]{0:T(1024)S(1)} %pad_clamp_fusion) | copy-start | bytes 12292
  76.4 1.0 copy-start.5
  85.7 35.6 %copy-start.18 = (bf16[128,1024]{1,0:T(8,128)(2,1)S(1)}, bf16[128,1024]{1,0:T(8,128)(2,1)}, u32[]{:S(2)}) copy-start(bf16[128,1024]{1,0:T(8,128)(2,1)} %param.30) | copy-start | bytes 786436
  125.0 1.2 copy-start.7
  125.0 1.2 copy-start.19
  125.0 2.8 %copy-start.30 = (pred[2,16]{1,0:T(4,128)(4,1)S(1)}, pred[2,16]{1,0:T(4,128)(4,1)}, u32[]{:S(2)}) copy-start(pred[2,16]{1,0:T(4,128)(4,1)} %iota_compare_fusion.2) | copy-start | bytes 100
  125.0 2.9 %copy-start.12 = (f32[2,16,16,64]{3,2,1,0:T(8,128)S(1)}, f32[2,16,16,64]{3,2,1,0:T(8,128)}, u32[]{:S(2)}) copy-start(f32[2,16,16,64]{3,2,1,0:T(8,128)} %reshape.403) | copy-start | bytes 393220
  125.0 2.9 %copy-start.13 = (f32[2,16,16,64]{3,2,1,0:T(8,128)S(1)}, f32[2,16,16,64]{3,2,1,0:T(8,128)}, u32[]{:S(2)}) copy-start(f32[2,16,16,64]{3,2,1,0:T(8,128)} %reshape.404) | copy-start | bytes 393220
  126.3 2.9 %slice-start = ((f32[416,1024]{1,0:T(8,128)}), f32[384,1024]{1,0:T(8,128)S(1)}, s32[]{:S(2)}) async-start(f32[416,1024]{1,0:T(8,128)} %copy-done.7), calls=%async_computation.6 | async-start | bytes 3145728 | tf_op jit(solution)/shard_map/slice | solution.py:182
  139.7 2.1 copy-start.3
  149.7 2.1 copy-start.3
  159.8 2.1 copy-start.3
  169.8 2.1 copy-start.3
  179.9 2.1 copy-start.3
  189.9 2.1 copy-start.3
  197.9 3.7 %copy-start.6 = (f32[2,64,16,64]{3,2,1,0:T(8,128)S(1)}, f32[2,64,16,64]{3,2,1,0:T(8,128)}, u32[]{:S(2)}) copy-start(f32[2,64,16,64]{3,2,1,0:T(8,128)} %copy-done.5) | copy-start | bytes 1572868
  201.2 1.0 copy-start.11
  204.2 12.2 %copy-start.14 = (f32[2,16,16,64]{3,2,1,0:T(8,128)S(1)}, f32[2,16,16,64]{3,2,1,0:T(8,128)}, u32[]{:S(2)}) copy-start(f32[2,16,16,64]{3,2,1,0:T(8,128)} %get-tuple-element.190) | copy-start | bytes 393220
  205.5 12.2 %copy-start.9 = (f32[2,16,16,64]{3,2,1,0:T(8,128)S(1)}, f32[2,16,16,64]{3,2,1,0:T(8,128)}, u32[]{:S(2)}) copy-start(f32[2,16,16,64]{3,2,1,0:T(8,128)} %get-tuple-element.189) | copy-start | bytes 393220
  205.5 12.2 %copy-start.10 = (f32[2,16,16,64]{3,2,1,0:T(8,128)S(1)}, f32[2,16,16,64]{3,2,1,0:T(8,128)}, u32[]{:S(2)}) copy-start(f32[2,16,16,64]{3,2,1,0:T(8,128)} %get-tuple-element.191) | copy-start | bytes 393220
  205.5 12.2 %copy-start.28 = (pred[16,16]{1,0:T(8,128)(4,1)S(1)}, pred[16,16]{1,0:T(8,128)(4,1)}, u32[]{:S(2)}) copy-start(pred[16,16]{1,0:T(8,128)(4,1)} %iota_compare_fusion.1) | copy-start | bytes 772
  205.5 29.9 %all-to-all-start.2 = ((f32[2,64,1024]{2,0,1:T(2,128)}), f32[2,64,1024]{2,0,1:T(2,128)S(1)}, u32[]{:S(2)}, u32[]{:S(2)}) async-start(f32[2,64,1024]{2,0,1:T(2,128)} %reshape.497), calls=%async_computation.2 | async-start | bytes 1048576 | tf_op jit(solution)/shard_map/all_to_all | solution.py:224
  216.4 2.5 %copy-start.4 = (f32[6,64,16,64]{3,1,2,0:T(8,128)S(1)}, f32[6,64,16,64]{3,1,2,0:T(8,128)}, u32[]{:S(2)}) copy-start(f32[6,64,16,64]{3,1,2,0:T(8,128)} %get-tuple-element.79) | copy-start | bytes 4718596
  229.2 1.6 copy-start.26
  229.2 1.6 copy-start.27
  235.8 2.4 copy-start.1
Sparse Core Ops, SparseCore 0:
  36.2 38.7 all-gather.4
  76.7 44.5 all-gather.2
where the time goes:
time: 246 us; the launch traced here: 245 us
  waiting for transfers between devices  54.8 us (22%)
  local copies, waits for them, and re-layouts  52.2 us (21%)
  matrix products  46.3 us (19%)
  other arithmetic  43.6 us (18%)
  starting transfers between devices  33.1 us (13%)
  between operations  14.8 us (6%)
    all_gather x1, waiting for transfers between devices, project(): lax.all_gather(decay_mixed_input, 'tp', axis=1, tiled=True)  33.6 us
    mul x6, other arithmetic, one_block(): keys_scaled = address_vectors_all * jnp.exp(middle - inclusive)  15 us
    all_to_all x1, starting transfers between devices, local(): lax.all_to_all(ordered_shift, 'rep', split_axis=0, concat_axis=1, tiled=T...  13 us
    dot_general x7, matrix products, one_block(): jnp.einsum('thi,hij->thj', accept_vectors_all * jnp.exp(exclusive), threa...  11.9 us
    all_to_all x1, starting transfers between devices, local(): lax.all_to_all(ret_state, 'rep', split_axis=1, concat_axis=0, tiled=True)  10.8 us
    dot_general x7, matrix products, one_block(): jnp.einsum('thi,shi->hts', recept_scaled, keys_scaled, precision=HIGH)  8.27 us
    dot_general x1, matrix products, project(): jnp.dot(lax.all_gather(mixed_value, 'tp', axis=1, tiled=True), content_ma...  8.09 us
    another operation x7, other arithmetic, one_block(): inclusive = jnp.cumsum(rate_b, axis=0)  8.08 us
  transfers between devices with their start and end apart: 6, of which 4 were waited for; matrix products, arithmetic and copies ran while one was open for 20% of the time, Pallas kernels for 0%

commit v1 on v0

v1 whole, which is shorter than its diff:
```python
import jax
import jax.numpy as jnp
from jax import lax
from jax.experimental import pallas as pl
from jax.experimental.pallas import tpu as pltpu
from jax.sharding import PartitionSpec as P

SPAN = 64
DRAFT = 16
EPS = 0.00064
REP = 64
TP = 4
WID = 1024
TAIL = 384
HALF = 192
LATE = 48
ROWS = HALF + LATE
PIECE = 48
CHUNK = 32
PAIRS = 8
RANK = 128
F32 = jnp.float32
BF16 = jnp.bfloat16
MESH = pl.DeviceIdType.MESH

ITEMS = (
    ("x", 0, 48),
    ("x", 48, 48),
    ("x", 96, 48),
    ("x", 144, 48),
    ("p", 0, 192),
    ("x", 192, 16),
    ("x", 208, 32),
    ("p", 192, 48),
)
RELAY_RIGHT = (0, 2, 4, 5, 7)


def iota(shape, dim):
    return lax.broadcasted_iota(jnp.int32, shape, dim)


def nt(a, b):
    return lax.dot_general(a, b, (((1,), (1,)), ((), ())), preferred_element_type=F32)


def tn(a, b):
    return lax.dot_general(a, b, (((0,), (0,)), ((), ())), preferred_element_type=F32)


def mm(a, b):
    return jnp.dot(a, b, preferred_element_type=F32)


def owner_tables(own_ref, spans_ref, adm_ref, perm_ref):
    hot = (iota((128, 128), 0) == own_ref[...]).astype(F32)
    row = iota((8, 128), 0)
    long_q = (spans_ref[...] > DRAFT).astype(F32)
    facts = jnp.where(row == 0, long_q, jnp.where(row == 1, adm_ref[...].astype(F32), 0.0))
    by_slot = mm(facts.astype(BF16), hot.astype(BF16))
    perm_ref[...] = hot.T
    dealt = jnp.concatenate([perm_ref[pl.ds(0, 64, stride=2), :], perm_ref[pl.ds(1, 64, stride=2), :]], axis=0)
    return dealt, by_slot


def fact(by_slot, row, slot):
    pick = iota((8, 128), 1) == slot
    here = jnp.where(pick & (iota((8, 128), 0) == row), by_slot, 0.0)
    return jnp.sum(jnp.sum(here, axis=1, keepdims=True), axis=0, keepdims=True)


def greet_rep(barrier, g, t):
    def one(d, _):
        pl.semaphore_signal(barrier, inc=1, device_id=(lax.rem(g + d, REP), t), device_id_type=MESH)
        return 0

    lax.fori_loop(1, REP, one, 0)


def scatter_rep(src, dst, send, recv, g, t):
    def one(d, _):
        to = lax.rem(g + d, REP)
        pltpu.make_async_remote_copy(
            src_ref=src.at[to],
            dst_ref=dst.at[g],
            send_sem=send,
            recv_sem=recv,
            device_id=(to, t),
            device_id_type=MESH,
        ).start()
        return 0

    lax.fori_loop(1, REP, one, 0)


def wait_rep(buf, sem):
    part = buf.at[pl.ds(0, REP - 1)]
    pltpu.make_async_copy(part, part, sem).wait()


def mixed(x, prev, share):
    return x + (prev - x) * share


def gather_kernel(
    x_ref, gx_ref, km_ref, p0_ref, mc_ref, mf_ref, own_ref, spans_ref, adm_ref, w_hbm, sh_hbm,
    got_ref, vt_ref, lt_ref, vl_ref, ll_ref, first_ref,
    w_ref, sh_ref, perm_ref, wide_ref, sbuf, pbuf, pgot, xv_ref, part_ref, xin, pin, xg, pg, acc, vh, lh,
    w_sem, sh_sem, st_send, st_recv, p_send, p_recv, pair_send, pair_recv,
    right_send, left_recv, left_send, right_recv, hop_send, hop_recv, back_send, back_recv,
):
    g, t = lax.axis_index("rep"), lax.axis_index("tp")
    core = lax.rem(g, 2)
    mate = g + 1 - 2 * core
    right, left, far = lax.rem(t + 1, TP), lax.rem(t + 3, TP), lax.rem(t + 2, TP)
    mine = pl.multiple_of(core * HALF, 16)
    other = pl.multiple_of((1 - core) * HALF, 16)

    def w_copy(k):
        rows = pl.ds(k * WID, WID)
        return pltpu.make_async_copy(w_hbm.at[rows], w_ref.at[rows], w_sem.at[k])

    sh_copy = pltpu.make_async_copy(sh_hbm.at[pl.ds(pl.multiple_of(t * WID, WID), WID)], sh_ref, sh_sem)
    sh_copy.start()
    for k in range(TP):
        w_copy(k).start()

    barrier = pltpu.get_barrier_semaphore()
    greet_rep(barrier, g, t)
    for d in range(1, TP):
        pl.semaphore_signal(barrier, inc=1, device_id=(g, lax.rem(t + d, TP)), device_id_type=MESH)

    dealt, by_slot = owner_tables(own_ref, spans_ref, adm_ref, perm_ref)
    dealt = dealt.astype(BF16)
    long_own = fact(by_slot, 0, 2 * g) > 0.5

    sent = nt(dealt, p0_ref[...])
    wide_ref[...] = jnp.zeros_like(wide_ref)
    wide_ref[pl.ds(0, 64, stride=8), 0:16] = sent[0:64]
    wide_ref[pl.ds(1, 64, stride=8), 0:16] = sent[64:128]
    pbuf[...] = wide_ref[0:512, :].astype(BF16).reshape(64, 8, 128)
    pgot[g] = pbuf[g]
    for c in range(8):
        rows = mm(dealt, km_ref[pl.ds(c, 128, stride=8), :].astype(BF16))
        wide_ref[pl.ds(c, 64, stride=16), :] = rows[0:64]
        wide_ref[pl.ds(8 + c, 64, stride=16), :] = rows[64:128]
    sbuf[...] = wide_ref[...].astype(BF16).reshape(64, 16, 128)
    got_ref[g] = sbuf[g]

    mc, mf = mc_ref[...], mf_ref[...]
    sh_copy.wait()

    def mix_rows(j, _):
        r0 = pl.multiple_of(j * PIECE, 16)
        x = x_ref[pl.ds(r0, PIECE), :].astype(F32)
        ahead = x_ref[pl.ds(pl.multiple_of(jnp.maximum(r0 - 16, 0), 16), 16), :].astype(F32)
        prev = jnp.where(iota((PIECE, WID), 0) == 0, ahead[15:16], pltpu.roll(x, 1, 0))
        xv_ref[pl.ds(r0, PIECE), :] = mixed(x, prev, mc).astype(BF16)
        part_ref[pl.ds(r0, PIECE), :] = mm(mixed(x, prev, mf).astype(BF16), sh_ref[...]).astype(BF16)
        return 0

    lax.fori_loop(0, TAIL // PIECE, mix_rows, 0)

    pl.semaphore_wait(barrier, REP - 1 + TP - 1)

    def pair_copy(j):
        if j < 4:
            src, dst = xv_ref.at[pl.ds(other + j * PIECE, PIECE)], xin.at[pl.ds(j * PIECE, PIECE)]
        else:
            src, dst = part_ref.at[pl.ds(other, HALF)], pin
        return pltpu.make_async_remote_copy(
            src_ref=src,
            dst_ref=dst,
            send_sem=pair_send.at[j],
            recv_sem=pair_recv.at[j],
            device_id=(mate, t),
            device_id_type=MESH,
        )

    def part_of(item, source):
        kind, r0, n = ITEMS[item]
        return (xg if kind == "x" else pg).at[source, pl.ds(r0, n)]

    def move(item, source, to, send, recv):
        return pltpu.make_async_remote_copy(
            src_ref=part_of(item, source),
            dst_ref=part_of(item, source),
            send_sem=send.at[item],
            recv_sem=recv.at[item],
            device_id=(g, to),
            device_id_type=MESH,
        )

    def give(item):
        move(item, t, right, right_send, left_recv).start()
        move(item, t, left, left_send, right_recv).start()

    for j in range(5):
        pair_copy(j).start()
    scatter_rep(pbuf, pgot, p_send, p_recv, g, t)
    for j in range(4):
        pair_copy(j).wait_recv()
        rows = pl.ds(j * PIECE, PIECE)
        xg[t, rows, :] = jnp.where(long_own, xv_ref[pl.ds(mine + j * PIECE, PIECE), :], xin[rows, :])
        give(j)
    pair_copy(4).wait_recv()
    pg[t, 0:HALF, :] = jnp.where(long_own, part_ref[pl.ds(mine, HALF), :], pin[...])
    give(4)
    scatter_rep(sbuf, got_ref, st_send, st_recv, g, t)

    wait_rep(pgot, p_recv)
    wide_ref[0:512, :] = pgot[...].reshape(512, 128).astype(F32)
    spread = (iota((128, WID), 1) // SPAN == iota((128, WID), 0)).astype(BF16)
    own_lane = iota((64, WID), 1) % SPAN == iota((64, WID), 0)
    before = []
    for s in range(2):
        vals = mm(wide_ref[pl.ds(s, 64, stride=8), :].astype(BF16), spread)
        before.append(jnp.sum(jnp.where(own_lane, vals, 0.0), axis=0, keepdims=True))
    final = x_ref[TAIL - 16 : TAIL, :].astype(F32)[15:16]
    firsts = [jnp.where(long_own, final, before[0]), before[1]]
    row8 = iota((8, WID), 0)
    first_ref[...] = jnp.where(row8 == 0, firsts[0], firsts[1])
    head = x_ref[0:16, :].astype(F32)
    cur = [gx_ref[0:16, :].astype(F32), gx_ref[16:32, :].astype(F32), head]
    row16 = iota((16, WID), 0)
    ahead = [jnp.where(row16 == 0, f, pltpu.roll(x, 1, 0)) for x, f in zip(cur, firsts + before[:1])]
    for s in range(3):
        xg[t, HALF + 16 * s : HALF + 16 * s + 16, :] = mixed(cur[s], ahead[s], mc).astype(BF16)
        pg[t, HALF + 16 * s : HALF + 16 * s + 16, :] = mm(
            mixed(cur[s], ahead[s], mf).astype(BF16), sh_ref[...]
        ).astype(BF16)
    for item in range(5, 8):
        give(item)

    def product(source, add):
        def tile(n, _):
            cols = pl.ds(pl.multiple_of(n * 256, 256), 256)
            out = mm(xg[source], w_ref[pl.ds(pl.multiple_of(source * WID, WID), WID), cols])
            acc[:, cols] = acc[:, cols] + out if add else out
            return 0

        lax.fori_loop(0, WID // 256, tile, 0)

    for k in range(TP):
        w_copy(k).wait()
    product(t, False)
    for item in range(8):
        move(item, left, right, right_send, left_recv).wait_recv()
        if item in RELAY_RIGHT:
            move(item, left, right, hop_send, hop_recv).start()
        move(item, right, left, left_send, right_recv).wait_recv()
        if item not in RELAY_RIGHT:
            move(item, right, left, hop_send, hop_recv).start()
    product(left, True)
    product(right, True)
    for item in range(8):
        move(item, far, right, hop_send, hop_recv).wait_recv()
    low = jnp.tanh(pg[0].astype(F32) + pg[1].astype(F32) + pg[2].astype(F32) + pg[3].astype(F32)).astype(BF16)
    lh[...] = low[0:HALF]
    ll_ref[...] = low[HALF:ROWS]
    lt_ref[pl.ds(mine, HALF), :] = low[0:HALF]
    product(far, True)
    vh[...] = acc[0:HALF, :].astype(BF16)

    def back_copy(src, dst, k):
        return pltpu.make_async_remote_copy(
            src_ref=src,
            dst_ref=dst.at[pl.ds(mine, HALF)],
            send_sem=back_send.at[k],
            recv_sem=back_recv.at[k],
            device_id=(mate, t),
            device_id_type=MESH,
        )

    backs = [back_copy(lh, lt_ref, 0), back_copy(vh, vt_ref, 1)]
    for b in backs:
        b.start()
    vt_ref[pl.ds(mine, HALF), :] = vh[...]
    vl_ref[...] = acc[HALF:ROWS, :].astype(BF16)
    wait_rep(got_ref, st_recv)
    wait_rep(pbuf, p_send)
    wait_rep(sbuf, st_send)
    for j in range(5):
        pair_copy(j).wait_send()
    for item in range(8):
        move(item, t, right, right_send, left_recv).wait_send()
        move(item, t, left, left_send, right_recv).wait_send()
        move(item, far, right, hop_send, hop_recv).wait_send()
    for b in backs:
        b.wait()
    vt_ref[0:16, :] = jnp.where(row16 == 0, vl_ref[32:33, :], vt_ref[0:16, :])
    lt_ref[0:16, :] = jnp.where(iota((16, RANK), 0) == 0, ll_ref[32:33, :], lt_ref[0:16, :])


def halves(a):
    low = iota(a.shape, 1) < SPAN
    zero = jnp.zeros_like(a)
    return jnp.concatenate([jnp.where(low, a, zero), jnp.where(low, zero, a)], axis=0)


def lanes(p):
    return slice(128 * p, 128 * p + 128)


def running(log, n):
    tri = (iota((n, n), 0) >= iota((n, n), 1)).astype(BF16)
    hi = log.astype(BF16)
    lo = (log - hi.astype(F32)).astype(BF16)
    return mm(tri, hi) + mm(tri, lo)


def answers(r, k, v, incl, log, boost, states, heads_sum, n):
    excl = incl - log
    mid = incl[n // 2 : n // 2 + 1]
    q = (r * jnp.exp(jnp.minimum(excl - mid, 80.0))).astype(BF16)
    kk = (k * jnp.exp(jnp.minimum(mid - incl, 80.0))).astype(BF16)
    ri = (r * jnp.exp(excl)).astype(BF16)
    own = (r * boost * k).astype(BF16)
    gain = mm(jnp.concatenate([own[:, lanes(p)] for p in range(PAIRS)], axis=0), heads_sum)
    strict = iota((2 * n, n), 0) % n > iota((2 * n, n), 1)
    low = iota((n, 128), 1) < SPAN
    out = []
    for p in range(PAIRS):
        c = lanes(p)
        score = jnp.where(strict, nt(halves(q[:, c]), kk[:, c]), 0.0).astype(BF16)
        both = mm(score, v[:, c])
        y = jnp.where(low, both[0:n], both[n : 2 * n])
        y = y + nt(ri[:, c], states[p].astype(BF16))
        out.append(y + gain[n * p : n * p + n] * v[:, c].astype(F32))
    return jnp.concatenate(out, axis=0)


def normed(y, heads_sum, scale, shift, n):
    hi = y.astype(BF16)
    lo = (y - hi.astype(F32)).astype(BF16)
    center = y - (mm(hi, heads_sum) + mm(lo, heads_sum)) * (1.0 / SPAN)
    spread = mm((center * center).astype(BF16), heads_sum) * (1.0 / SPAN)
    o = center * lax.rsqrt(spread + EPS)
    return jnp.concatenate(
        [o[n * p : n * p + n] * scale[:, lanes(p)] + shift[:, lanes(p)] for p in range(PAIRS)], axis=1
    )


def mix_kernel(
    rt_ref, kt_ref, gx_ref, gr_ref, gk_ref, vt_ref, lt_ref, vl_ref, ll_ref, got_ref, first_ref,
    ex_ref, anchor_ref, boost_ref, scale_ref, shift_ref, own_ref, spans_ref, adm_ref,
    tail_ref, draft_ref, state_ref, prior_ref,
    perm_ref, wide_ref, st_ref, sbuf, sgot, ebuf, egot, s_send, s_recv, e_send, e_recv,
):
    g, t = lax.axis_index("rep"), lax.axis_index("tp")
    barrier = pltpu.get_barrier_semaphore()
    greet_rep(barrier, g, t)
    dealt, by_slot = owner_tables(own_ref, spans_ref, adm_ref, perm_ref)
    long_own = fact(by_slot, 0, 2 * g) > 0.5
    boost, scale, shift = boost_ref[...], scale_ref[...], shift_ref[...]
    anchor = anchor_ref[...]
    same = iota((128, 128), 0) // SPAN == iota((128, 128), 1) // SPAN
    heads_sum = same.astype(BF16)

    spread = (iota((128, WID), 1) // SPAN == iota((128, WID), 0)).astype(BF16)
    own_lane = iota((64, WID), 1) % SPAN == iota((64, WID), 0)
    row16 = iota((DRAFT, WID), 0)
    counts = []
    wide_ref[0:512, :] = jnp.zeros((512, 128), F32)
    for s in range(2):
        count = fact(by_slot, 1, 2 * g + s).astype(jnp.int32)
        counts.append(count)
        rows = gx_ref[DRAFT * s : DRAFT * s + DRAFT, :].astype(F32)
        edge = jnp.sum(jnp.where(row16 == count - 1, rows, 0.0), axis=0, keepdims=True)
        edge = jnp.where(count > 0, edge, first_ref[s : s + 1, :])
        wide_ref[pl.ds(s, 64, stride=8), :] = nt(jnp.where(own_lane, edge, 0.0).astype(BF16), spread)
    ebuf[...] = wide_ref[0:512, :].astype(BF16).reshape(64, 8, 128)
    egot[g] = ebuf[g]

    wide_ref[...] = got_ref[...].reshape(1024, 128).astype(F32)
    for s in range(2):
        for p in range(PAIRS):
            rows = wide_ref[pl.ds(8 * s + p, 64, stride=16), :]
            st_ref[s, p] = halves(rows).T

    pl.semaphore_wait(barrier, REP - 1)
    scatter_rep(ebuf, egot, e_send, e_recv, g, t)

    st0 = [st_ref[0, p] for p in range(PAIRS)]

    def chunk(i, _):
        rows = pl.ds(pl.multiple_of(i * CHUNK, 16), CHUNK)
        log = -jnp.exp(anchor + mm(lt_ref[rows, :], ex_ref[...]))
        r, k, v = rt_ref[rows, :].astype(F32), kt_ref[rows, :].astype(F32), vt_ref[rows, :]
        incl = running(log, CHUNK)
        states = [st_ref[2, p] for p in range(PAIRS)]
        y = answers(r, k, v, incl, log, boost, states, heads_sum, CHUNK)
        last = incl[CHUNK - 1 : CHUNK]
        kd = (k * jnp.exp(last - incl)).astype(BF16)
        keep = jnp.exp(last)
        for p in range(PAIRS):
            c = lanes(p)
            st_ref[2, p] = states[p] * keep[:, c] + jnp.where(same, tn(v[:, c], kd[:, c]), 0.0)
        o = normed(y, heads_sum, scale, shift, CHUNK)
        tail_ref[rows, :] = jnp.where(long_own, o, 0.0).astype(BF16)
        return 0

    for p in range(PAIRS):
        st_ref[2, p] = st_ref[0, p]
    lax.fori_loop(0, TAIL // CHUNK, chunk, 0)

    for s in range(2):
        rows = slice(DRAFT * s, DRAFT * s + DRAFT)
        log = -jnp.exp(anchor + mm(ll_ref[rows, :], ex_ref[...]))
        r, k, v = gr_ref[rows, :].astype(F32), gk_ref[rows, :].astype(F32), vl_ref[rows, :]
        incl = running(log, DRAFT)
        if s == 0:
            states = [jnp.where(long_own, st_ref[2, p], st_ref[0, p]) for p in range(PAIRS)]
        else:
            states = [st_ref[1, p] for p in range(PAIRS)]
        y = answers(r, k, v, incl, log, boost, states, heads_sum, DRAFT)
        draft_ref[rows, :] = normed(y, heads_sum, scale, shift, DRAFT).astype(BF16)
        taken = row16 < counts[s]
        upto = jnp.sum(jnp.where(taken, log, 0.0), axis=0, keepdims=True)
        weight = jnp.where(taken, jnp.exp(jnp.where(taken, upto - incl, 0.0)), 0.0)
        kd = (k * weight).astype(BF16)
        keep = jnp.exp(upto)
        for p in range(PAIRS):
            c = lanes(p)
            end = (states[p] * keep[:, c] + jnp.where(same, tn(v[:, c], kd[:, c]), 0.0)).T
            wide_ref[pl.ds(8 * s + p, 64, stride=16), :] = end[0:64] + end[64:128]
    sbuf[...] = wide_ref[...].astype(BF16).reshape(64, 16, 128)
    sgot[g] = sbuf[g]
    scatter_rep(sbuf, sgot, s_send, s_recv, g, t)

    hot = dealt.astype(BF16)
    wait_rep(egot, e_recv)
    wide_ref[0:512, :] = egot[...].reshape(512, 128).astype(F32)
    edges = jnp.concatenate([wide_ref[pl.ds(0, 64, stride=8), :], wide_ref[pl.ds(1, 64, stride=8), :]], axis=0)
    prior_ref[...] = tn(edges.astype(BF16), hot)[0:16].astype(BF16)
    by_req = dealt.T.astype(BF16)
    wait_rep(sgot, s_recv)
    wide_ref[...] = sgot[...].reshape(1024, 128).astype(F32)
    for c in range(8):
        rows = jnp.concatenate(
            [wide_ref[pl.ds(c, 64, stride=16), :], wide_ref[pl.ds(8 + c, 64, stride=16), :]], axis=0
        )
        state_ref[pl.ds(c, 128, stride=8), :] = mm(by_req, rows.astype(BF16))
    wait_rep(ebuf, e_send)
    wait_rep(sbuf, s_send)


VM = pl.BlockSpec(memory_space=pltpu.VMEM)
ANY = pl.BlockSpec(memory_space=pl.ANY)
DMA = pltpu.SemaphoreType.DMA


def local(
    suffix_source, suffix_accept, suffix_address, guess_lane_source, guess_lane_accept, guess_lane_address,
    content_map, forget_shrink_map, forget_expand_map, forget_lane_anchor, present_boost,
    content_blend_share, forget_blend_share, lane_normal_scale, lane_normal_shift,
    kernel_memory_saved, prior_source_saved, lane_owner, request_spans, admitted_guesses,
):
    gx = guess_lane_source.reshape(2 * DRAFT, WID)
    small = [a.reshape(1, 128) for a in (lane_owner, request_spans, admitted_guesses)]
    sds = jax.ShapeDtypeStruct
    got, vt, lt, vl, ll, first = pl.pallas_call(
        gather_kernel,
        name="gather_project",
        out_shape=(
            sds((REP, 16, 128), BF16),
            sds((TAIL, WID), BF16),
            sds((TAIL, RANK), BF16),
            sds((LATE, WID), BF16),
            sds((LATE, RANK), BF16),
            sds((8, WID), F32),
        ),
        in_specs=[VM] * 9 + [ANY, ANY],
        out_specs=(VM,) * 6,
        scratch_shapes=[
            pltpu.VMEM((TP * WID, WID), BF16),
            pltpu.VMEM((WID, RANK), BF16),
            pltpu.VMEM((128, 128), F32),
            pltpu.VMEM((1024, 128), F32),
            pltpu.VMEM((REP, 16, 128), BF16),
            pltpu.VMEM((REP, 8, 128), BF16),
            pltpu.VMEM((REP, 8, 128), BF16),
            pltpu.VMEM((TAIL, WID), BF16),
            pltpu.VMEM((TAIL, RANK), BF16),
            pltpu.VMEM((HALF, WID), BF16),
            pltpu.VMEM((HALF, RANK), BF16),
            pltpu.VMEM((TP, ROWS, WID), BF16),
            pltpu.VMEM((TP, ROWS, RANK), BF16),
            pltpu.VMEM((ROWS, WID), F32),
            pltpu.VMEM((HALF, WID), BF16),
            pltpu.VMEM((HALF, RANK), BF16),
            DMA((TP,)), DMA, DMA, DMA, DMA, DMA, DMA((5,)), DMA((5,)),
            DMA((8,)), DMA((8,)), DMA((8,)), DMA((8,)), DMA((8,)), DMA((8,)), DMA((2,)), DMA((2,)),
        ],
        compiler_params=pltpu.CompilerParams(
            collective_id=0, has_side_effects=True, vmem_limit_bytes=48 << 20
        ),
    )(
        suffix_source.reshape(TAIL, WID),
        gx,
        kernel_memory_saved.reshape(1024, 128),
        prior_source_saved.reshape(128, 16).T,
        content_blend_share.reshape(1, WID),
        forget_blend_share.reshape(1, WID),
        *small,
        content_map,
        forget_shrink_map,
    )
    tail, draft, state, prior = pl.pallas_call(
        mix_kernel,
        name="mix_return",
        out_shape=(
            sds((TAIL, WID), BF16),
            sds((2 * DRAFT, WID), BF16),
            sds((1024, 128), F32),
            sds((16, 128), BF16),
        ),
        in_specs=[VM] * 19,
        out_specs=(VM,) * 4,
        scratch_shapes=[
            pltpu.VMEM((128, 128), F32),
            pltpu.VMEM((1024, 128), F32),
            pltpu.VMEM((3, PAIRS, 128, 128), F32),
            pltpu.VMEM((REP, 16, 128), BF16),
            pltpu.VMEM((REP, 16, 128), BF16),
            pltpu.VMEM((REP, 8, 128), BF16),
            pltpu.VMEM((REP, 8, 128), BF16),
            DMA, DMA, DMA, DMA,
        ],
        compiler_params=pltpu.CompilerParams(
            collective_id=1, has_side_effects=True, vmem_limit_bytes=48 << 20
        ),
    )(
        suffix_accept.reshape(TAIL, WID),
        suffix_address.reshape(TAIL, WID),
        gx,
        guess_lane_accept.reshape(2 * DRAFT, WID),
        guess_lane_address.reshape(2 * DRAFT, WID),
        vt, lt, vl, ll, got, first,
        forget_expand_map,
        forget_lane_anchor.reshape(1, WID),
        present_boost.reshape(1, WID),
        lane_normal_scale.reshape(1, WID),
        lane_normal_shift.reshape(1, WID),
        *small,
    )
    return (
        tail.reshape(1, TAIL, WID),
        draft.reshape(2, DRAFT, WID),
        state.reshape(128, 1, WID),
        prior.T.reshape(128, 1, 16),
    )


def solution(mesh):
    rows, cols, chan = P("rep", None, "tp"), P(None, "tp"), P("tp")
    cache = P(None, "rep", "tp")
    return jax.shard_map(
        local,
        mesh=mesh,
        in_specs=(rows,) * 6 + (cols, P(), cols) + (chan,) * 6 + (cache, cache, P(), P(), P()),
        out_specs=(rows, rows, cache, cache),
        check_vma=False,
    )
```

time: 246 us -> 87.8 us (0.36)
  Pallas kernels: 0 us -> 75.5 us
  waiting for transfers between devices: 54.8 us -> 0 us
  matrix products: 46.3 us -> 0 us
  other arithmetic: 43.6 us -> 0 us
  local copies, waits for them, and re-layouts: 52.2 us -> 11.2 us
  starting transfers between devices: 33.1 us -> 0 us
  between operations: 14.8 us -> 0.79 us
    pallas_call x0 -> x2, Pallas kernels: none -> 75.5 us  [the longest x1 38.3 us: local(): pl.pallas_call(gather_kernel, name='gather_project', out_shape=(sds((REP,...]
    dot_general x30 -> x0, matrix products: 46.3 us -> none  [the longest x7 11.9 us: one_block(): jnp.einsum('thi,hij->thj', accept_vectors_all * jnp.exp(exclusive), threa...]
    all_gather x2 -> x0, waiting for transfers between devices: 33.6 us -> none  [the longest x1 33.6 us: project(): lax.all_gather(decay_mixed_input, 'tp', axis=1, tiled=True)]
    all_to_all x4 -> x0, starting transfers between devices: 33 us -> none  [the longest x1 13 us: local(): lax.all_to_all(ordered_shift, 'rep', split_axis=0, concat_axis=1, tiled=T...]
    all_to_all x4 -> x0, waiting for transfers between devices: 21.1 us -> none  [the longest x1 7.31 us: local(): lax.all_to_all(ordered_shift, 'rep', split_axis=0, concat_axis=1, tiled=T...]
    mul x7 -> x0, other arithmetic: 16.2 us -> none  [the longest x6 15 us: one_block(): keys_scaled = address_vectors_all * jnp.exp(middle - inclusive)]
    another operation x8 -> x0, other arithmetic: 9.44 us -> none  [the longest x7 8.08 us: one_block(): inclusive = jnp.cumsum(rate_b, axis=0)]
    gather x11 -> x0, local copies, waits for them, and re-layouts: 8.64 us -> none  [the longest x2 2.13 us: local(): ordered_state = kernel_memory_saved[lane_owner]]
  transfers between devices with their start and end apart: 6 -> 0, of which waited for: 4 -> 0; matrix products, arithmetic and copies ran while one was open for 20% -> 0% of each run, Pallas kernels for 0% -> 0%
where the time goes in v1:
time: 87.8 us; the launch traced here: 87.5 us
  Pallas kernels  75.5 us (86%)
  local copies, waits for them, and re-layouts  11.2 us (13%)
    pallas_call x1, Pallas kernels, local(): pl.pallas_call(gather_kernel, name='gather_project', out_shape=(sds((REP,...  38.3 us
    pallas_call x1, Pallas kernels, local(): pl.pallas_call(mix_kernel, name='mix_return', out_shape=(sds((TAIL, WID),...  37.2 us
    unnamed x42, local copies, waits for them, and re-layouts  11.2 us

profile of v1, /device:TPU:1, one launch (start us, length us, event | category | flops | bytes accessed | tf_op | source)
XLA Modules:
  0.0 87.5 jit_solution(17649501562433567076)
XLA Ops:
  0.6 0.0 copy-start.15
  0.6 0.0 copy-start.14
  0.7 0.0 copy-start.13
  0.7 0.0 copy-start.12
  0.7 0.0 copy-start
  0.7 1.2 %copy-done = bf16[4096,128]{1,0:T(8,128)(2,1)S(1)} copy-done((bf16[4096,128]{1,0:T(8,128)(2,1)S(1)}, bf16[4096,128]{1,0:T(8,128)(2,1)}, u32[]{:S(2)}) %copy-start) | copy-done | bytes 1048600
  1.9 0.0 copy-start.1
  1.9 1.1 %copy-done.1 = bf16[1,384,1024]{2,1,0:T(8,128)(2,1)S(1)} copy-done((bf16[1,384,1024]{2,1,0:T(8,128)(2,1)S(1)}, bf16[1,384,1024]{2,1,0:T(8,128)(2,1)}, u32[]{:S(2)}) %copy-start.1) | copy-done | bytes 786456
  3.1 0.0 copy-start.4
  3.1 1.0 %copy-done.4 = f32[128,1,1024]{2,1,0:T(1,128)S(1)} copy-done((f32[128,1,1024]{2,1,0:T(1,128)S(1)}, f32[128,1,1024]{2,1,0:T(1,128)}, u32[]{:S(2)}) %copy-start.4) | copy-done | bytes 524312
  4.1 0.0 copy-start.5
  4.1 0.8 copy-done.5
  4.9 0.0 copy-start.9
  4.9 0.7 copy-done.9
  5.6 0.0 copy-start.10
  5.6 0.7 copy-done.10
  6.3 0.0 copy-start.11
  6.3 0.7 copy-done.11
  7.0 0.0 copy-start.16
  7.0 0.7 copy-done.16
  7.7 0.0 copy-start.17
  7.7 0.7 copy-done.17
  8.3 0.0 copy-start.18
  8.3 0.7 copy-done.18
  9.0 0.0 copy-start.2
  9.0 0.0 copy-start.3
  9.0 0.0 copy-start.6
  9.0 0.0 copy-start.7
  9.0 0.0 copy-start.8
  9.0 38.3 %gather_project.1 = (bf16[64,16,128]{2,1,0:T(8,128)(2,1)S(1)}, bf16[384,1024]{1,0:T(8,128)(2,1)S(1)}, bf16[384,128]{1,0:T(8,128)(2,1)S(1)}, bf16[48,1024]{1,0:T(...) custom-call(bf16[384,1024]{1,0:T(8,128)(2,1)S(1)} %bitcast.25, bf16[32,1024]{1,0:T(8,128)(2,1)S(1)} %bitcast.31, ...), custom_call_target="tpu_custom_call" | custom-call | tf_op jit(solution)/shard_map/gather_project/pallas_call | solution.py:462
  47.3 0.0 copy-done.15
  47.3 0.0 copy-done.14
  47.3 0.0 copy-done.13
  47.3 0.0 copy-done.12
  47.3 0.0 copy-done.2
  47.3 0.0 copy-done.3
  47.4 0.0 copy-done.6
  47.4 0.0 copy-done.7
  47.4 0.0 copy-done.8
  47.4 37.2 %mix_return.1 = (bf16[384,1024]{1,0:T(8,128)(2,1)S(1)}, bf16[32,1024]{1,0:T(8,128)(2,1)S(1)}, f32[1024,128]{1,0:T(8,128)S(1)}, bf16[16,128]{1,0:T(8,128)(2,1)S(1)}) custom-call(bf16[384,1024]{1,0:T(8,128)(2,1)S(1)} %bitcast.27, bf16[384,1024]{1,0:T(8,128)(2,1)S(1)} %bitcast.28, bf16[32,1024]{1,0:T(8,128)(2,1)S(1)} %bitcast.32, ...), custom_call_target="tpu_custom_call" | custom-call | tf_op jit(solution)/shard_map/mix_return/pallas_call | solution.py:509
  84.6 0.9 %copy.29 = bf16[1,384,1024]{2,1,0:T(8,128)(2,1)} copy(bf16[1,384,1024]{2,1,0:T(8,128)(2,1)S(1)} %bitcast.26) | data formatting | bytes 1572864
  85.5 0.6 copy.30
  86.1 0.8 copy.31
  86.9 0.6 copy.32
Async XLA Ops:
  0.6 46.7 %copy-start.15 = (f32[1024]{0:T(1024)S(1)}, f32[1024]{0:T(1024)}, u32[]{:S(2)}) copy-start(f32[1024]{0:T(1024)} %param.34) | copy-start | bytes 12292
  0.6 46.7 %copy-start.14 = (f32[1024]{0:T(1024)S(1)}, f32[1024]{0:T(1024)}, u32[]{:S(2)}) copy-start(f32[1024]{0:T(1024)} %param.33) | copy-start | bytes 12292
  0.7 46.7 %copy-start.13 = (f32[1024]{0:T(1024)S(1)}, f32[1024]{0:T(1024)}, u32[]{:S(2)}) copy-start(f32[1024]{0:T(1024)} %param.30) | copy-start | bytes 12292
  0.7 46.7 %copy-start.12 = (f32[1024]{0:T(1024)S(1)}, f32[1024]{0:T(1024)}, u32[]{:S(2)}) copy-start(f32[1024]{0:T(1024)} %param.29) | copy-start | bytes 12292
  0.7 1.2 %copy-start = (bf16[4096,128]{1,0:T(8,128)(2,1)S(1)}, bf16[4096,128]{1,0:T(8,128)(2,1)}, u32[]{:S(2)}) copy-start(bf16[4096,128]{1,0:T(8,128)(2,1)} %sh_hbm.1) | copy-start | bytes 3145732
  1.9 1.1 %copy-start.1 = (bf16[1,384,1024]{2,1,0:T(8,128)(2,1)S(1)}, bf16[1,384,1024]{2,1,0:T(8,128)(2,1)}, u32[]{:S(2)}) copy-start(bf16[1,384,1024]{2,1,0:T(8,128)(2,1)} %param.20) | copy-start | bytes 2359300
  3.1 1.0 %copy-start.4 = (f32[128,1,1024]{2,1,0:T(1,128)S(1)}, f32[128,1,1024]{2,1,0:T(1,128)}, u32[]{:S(2)}) copy-start(f32[128,1,1024]{2,1,0:T(1,128)} %param.35) | copy-start | bytes 1572868
  4.1 0.8 copy-start.5
  4.9 0.7 copy-start.9
  5.6 0.7 copy-start.10
  6.3 0.7 copy-start.11
  7.0 0.7 copy-start.16
  7.7 0.7 copy-start.17
  8.3 0.7 copy-start.18
  9.0 38.4 %copy-start.2 = (bf16[1,384,1024]{2,1,0:T(8,128)(2,1)S(1)}, bf16[1,384,1024]{2,1,0:T(8,128)(2,1)}, u32[]{:S(2)}) copy-start(bf16[1,384,1024]{2,1,0:T(8,128)(2,1)} %param.21) | copy-start | bytes 2359300
  9.0 38.4 %copy-start.3 = (bf16[1,384,1024]{2,1,0:T(8,128)(2,1)S(1)}, bf16[1,384,1024]{2,1,0:T(8,128)(2,1)}, u32[]{:S(2)}) copy-start(bf16[1,384,1024]{2,1,0:T(8,128)(2,1)} %param.22) | copy-start | bytes 2359300
  9.0 38.4 %copy-start.6 = (bf16[128,1024]{1,0:T(8,128)(2,1)S(1)}, bf16[128,1024]{1,0:T(8,128)(2,1)}, u32[]{:S(2)}) copy-start(bf16[128,1024]{1,0:T(8,128)(2,1)} %ex_ref.1) | copy-start | bytes 786436
  9.0 38.4 %copy-start.7 = (bf16[2,16,1024]{2,1,0:T(8,128)(2,1)S(1)}, bf16[2,16,1024]{2,1,0:T(8,128)(2,1)}, u32[]{:S(2)}) copy-start(bf16[2,16,1024]{2,1,0:T(8,128)(2,1)} %param.24) | copy-start | bytes 196612
  9.0 38.4 %copy-start.8 = (bf16[2,16,1024]{2,1,0:T(8,128)(2,1)S(1)}, bf16[2,16,1024]{2,1,0:T(8,128)(2,1)}, u32[]{:S(2)}) copy-start(bf16[2,16,1024]{2,1,0:T(8,128)(2,1)} %param.25) | copy-start | bytes 196612

commit v2 on v1

v2 whole, which is shorter than its diff:
```python
import jax
import jax.numpy as jnp
from jax import lax
from jax.experimental import pallas as pl
from jax.experimental.pallas import tpu as pltpu
from jax.sharding import PartitionSpec as P

SPAN = 64
DRAFT = 16
EPS = 0.00064
REP = 64
TP = 4
WID = 1024
TAIL = 384
HALF = 192
LATE = 48
ROWS = HALF + LATE
PIECE = 48
CHUNK = 32
PAIRS = 8
RANK = 128
F32 = jnp.float32
BF16 = jnp.bfloat16
MESH = pl.DeviceIdType.MESH

SIDE = WID // 2
SPLIT = PAIRS // 2
STEPS = TAIL // CHUNK

ITEMS = (
    ("p", 0, 192),
    ("x", 0, 48),
    ("x", 48, 48),
    ("x", 96, 48),
    ("x", 144, 48),
    ("x", 192, 16),
    ("x", 208, 32),
    ("p", 192, 48),
)
RELAY_RIGHT = (0, 1, 3, 5, 7)


def iota(shape, dim):
    return lax.broadcasted_iota(jnp.int32, shape, dim)


def nt(a, b):
    return lax.dot_general(a, b, (((1,), (1,)), ((), ())), preferred_element_type=F32)


def tn(a, b):
    return lax.dot_general(a, b, (((0,), (0,)), ((), ())), preferred_element_type=F32)


def mm(a, b):
    return jnp.dot(a, b, preferred_element_type=F32)


def owner_tables(own_ref, spans_ref, adm_ref, perm_ref):
    hot = (iota((128, 128), 0) == own_ref[...]).astype(F32)
    row = iota((8, 128), 0)
    long_q = (spans_ref[...] > DRAFT).astype(F32)
    facts = jnp.where(row == 0, long_q, jnp.where(row == 1, adm_ref[...].astype(F32), 0.0))
    by_slot = mm(facts.astype(BF16), hot.astype(BF16))
    perm_ref[...] = hot.T
    dealt = jnp.concatenate([perm_ref[pl.ds(0, 64, stride=2), :], perm_ref[pl.ds(1, 64, stride=2), :]], axis=0)
    return dealt, by_slot


def fact(by_slot, row, slot):
    pick = iota((8, 128), 1) == slot
    here = jnp.where(pick & (iota((8, 128), 0) == row), by_slot, 0.0)
    return jnp.sum(jnp.sum(here, axis=1, keepdims=True), axis=0, keepdims=True)


def greet_rep(barrier, g, t):
    def one(d, _):
        pl.semaphore_signal(barrier, inc=1, device_id=(lax.rem(g + d, REP), t), device_id_type=MESH)
        return 0

    lax.fori_loop(1, REP, one, 0)


def scatter_rep(src, dst, send, recv, g, t):
    def one(d, _):
        to = lax.rem(g + d, REP)
        pltpu.make_async_remote_copy(
            src_ref=src.at[to],
            dst_ref=dst.at[g],
            send_sem=send,
            recv_sem=recv,
            device_id=(to, t),
            device_id_type=MESH,
        ).start()
        return 0

    lax.fori_loop(1, REP, one, 0)


def wait_rep(buf, sem):
    part = buf.at[pl.ds(0, REP - 1)]
    pltpu.make_async_copy(part, part, sem).wait()


def mixed(x, prev, share):
    return x + (prev - x) * share


def halves(a):
    low = iota(a.shape, 1) < SPAN
    zero = jnp.zeros_like(a)
    return jnp.concatenate([jnp.where(low, a, zero), jnp.where(low, zero, a)], axis=0)


def lanes(p):
    return slice(128 * p, 128 * p + 128)


def stack(a, pairs):
    return jnp.concatenate([a[:, lanes(p)] for p in range(pairs)], axis=0)


def running(log, n):
    tri = (iota((n, n), 0) >= iota((n, n), 1)).astype(BF16)
    hi = log.astype(BF16)
    lo = (log - hi.astype(F32)).astype(BF16)
    return mm(tri, hi) + mm(tri, lo)


def column(row):
    hi = row.astype(BF16).astype(F32)
    rest = row - hi
    mid = rest.astype(BF16).astype(F32)
    low = rest - mid
    at = iota((16, 128), 0)
    parts = jnp.where(at == 0, hi, jnp.where(at == 1, mid, jnp.where(at == 2, low, 0.0)))
    return tn(parts.astype(BF16), jnp.ones((16, 128), BF16))


def scaled(r, k, incl, log, n):
    excl = incl - log
    mid = incl[n // 2 : n // 2 + 1]
    q = (r * jnp.exp(jnp.minimum(excl - mid, 80.0))).astype(BF16)
    kk = (k * jnp.exp(jnp.minimum(mid - incl, 80.0))).astype(BF16)
    return q, kk, (r * jnp.exp(excl)).astype(BF16)


def scored(q, kk, n):
    strict = iota((2 * n, n), 0) % n > iota((2 * n, n), 1)
    return jnp.where(strict, nt(halves(q), kk), 0.0).astype(BF16)


def normed(y, heads_sum, scale, shift, n, pairs):
    hi = y.astype(BF16)
    lo = (y - hi.astype(F32)).astype(BF16)
    center = y - (mm(hi, heads_sum) + mm(lo, heads_sum)) * (1.0 / SPAN)
    spread = mm((center * center).astype(BF16), heads_sum) * (1.0 / SPAN)
    o = center * lax.rsqrt(spread + EPS)
    return jnp.concatenate(
        [o[n * p : n * p + n] * scale[:, lanes(p)] + shift[:, lanes(p)] for p in range(pairs)], axis=1
    )


def mix_kernel(
    x_hbm, gx_hbm, km_hbm, p0_hbm, mc_hbm, mf_hbm, own_hbm, spans_hbm, adm_hbm, gr_hbm, gk_hbm, ex_hbm,
    anchor_hbm, boost_hbm, scale_hbm, shift_hbm, w_hbm, sh_hbm, rt_hbm, kt_hbm,
    tail_ref, draft_ref, state_ref, prior_ref,
    x_ref, gx_ref, km_ref, p0_ref, mc_ref, mf_ref, own_ref, spans_ref, adm_ref, gr_ref, gk_ref, ex_ref,
    anchor_ref, boost_ref, scale_ref, shift_ref, w_ref, sh_ref, rown, kown,
    perm_ref, wide_ref, sbuf, sgot, pbuf, pgot, xv_ref, part_ref, xin, pin, zsend, zpart, zin, zpin,
    xg, pg, acc, vh, lh, vl_ref, ll_ref, first_ref, vt_ref, lt_ref, rmate, kmate, st0_ref, stm_ref,
    sc_ref, ri_ref, gain_ref, kd_ref, keep_ref, st_ref, endm_ref, y_ref, o_ref, om_ref,
    dy_ref, dri_ref, du_ref, dk_ref, rbuf, rgot, ebuf, egot,
    in_sem, w_sem, st_send, st_recv, p_send, p_recv, e_send, e_recv, b_send, b_recv, mate_send, mate_recv,
    right_send, left_recv, left_send, right_recv, hop_send, hop_recv,
):
    g, t = lax.axis_index("rep"), lax.axis_index("tp")
    core = lax.rem(g, 2)
    mate = g + 1 - 2 * core
    right, left, far = lax.rem(t + 1, TP), lax.rem(t + 3, TP), lax.rem(t + 2, TP)
    mine = pl.multiple_of(core * HALF, 16)
    other = pl.multiple_of((1 - core) * HALF, 16)
    cols = pl.ds(pl.multiple_of(core * SIDE, 128), SIDE)
    mate_cols = pl.ds(pl.multiple_of((1 - core) * SIDE, 128), SIDE)

    own_rows = pl.ds(pl.multiple_of(t * WID, WID), WID)
    plain = (
        (x_hbm, x_ref), (mf_hbm, mf_ref), (mc_hbm, mc_ref), (sh_hbm.at[own_rows], sh_ref), (own_hbm, own_ref),
        (spans_hbm, spans_ref), (adm_hbm, adm_ref), (p0_hbm, p0_ref), (gx_hbm, gx_ref), (km_hbm, km_ref),
        (rt_hbm.at[:, cols], rown), (kt_hbm.at[:, cols], kown), (gr_hbm, gr_ref), (gk_hbm, gk_ref), (ex_hbm, ex_ref),
        (anchor_hbm, anchor_ref), (boost_hbm, boost_ref), (scale_hbm, scale_ref), (shift_hbm, shift_ref),
    )

    def in_copy(i):
        return pltpu.make_async_copy(plain[i][0], plain[i][1], in_sem.at[i])

    def w_copy(k):
        rows = pl.ds(k * WID, WID)
        return pltpu.make_async_copy(w_hbm.at[rows], w_ref.at[rows], w_sem.at[k])

    for i in range(len(plain)):
        in_copy(i).start()
    for k in range(TP):
        w_copy(k).start()

    barrier = pltpu.get_barrier_semaphore()
    greet_rep(barrier, g, t)
    for d in range(1, TP):
        pl.semaphore_signal(barrier, inc=1, device_id=(g, lax.rem(t + d, TP)), device_id_type=MESH)

    for i in range(4):
        in_copy(i).wait()
    mc, mf = mc_ref[...], mf_ref[...]

    def mix_rows(j, _):
        r0 = pl.multiple_of(j * PIECE, 16)
        x = x_ref[pl.ds(r0, PIECE), :].astype(F32)
        ahead = x_ref[pl.ds(pl.multiple_of(jnp.maximum(r0 - 16, 0), 16), 16), :].astype(F32)
        prev = jnp.where(iota((PIECE, WID), 0) == 0, ahead[15:16], pltpu.roll(x, 1, 0))
        xv_ref[pl.ds(r0, PIECE), :] = mixed(x, prev, mc).astype(BF16)
        part_ref[pl.ds(r0, PIECE), :] = mm(mixed(x, prev, mf).astype(BF16), sh_ref[...]).astype(BF16)
        return 0

    lax.fori_loop(0, TAIL // PIECE, mix_rows, 0)
    for i in range(4, len(plain)):
        in_copy(i).wait()
    pl.semaphore_wait(barrier, REP - 1 + TP - 1)

    moves = {
        0: (part_ref.at[pl.ds(other, HALF)], pin),
        5: (rt_hbm.at[:, mate_cols], rmate),
        6: (kt_hbm.at[:, mate_cols], kmate),
        7: (zsend, zin),
        8: (zpart, zpin),
        9: (lh, lt_ref.at[pl.ds(mine, HALF)]),
        10: (vh.at[:, mate_cols], vt_ref.at[pl.ds(mine, HALF)]),
        11: (st0_ref.at[pl.ds((1 - core) * SPLIT, SPLIT)], stm_ref),
        12: (st_ref, endm_ref),
        13: (o_ref, om_ref),
    }
    for j in range(4):
        moves[1 + j] = (xv_ref.at[pl.ds(other + j * PIECE, PIECE)], xin.at[pl.ds(j * PIECE, PIECE)])

    def to_mate(j):
        return pltpu.make_async_remote_copy(
            src_ref=moves[j][0],
            dst_ref=moves[j][1],
            send_sem=mate_send.at[j],
            recv_sem=mate_recv.at[j],
            device_id=(mate, t),
            device_id_type=MESH,
        )

    def part_of(item, source):
        kind, r0, n = ITEMS[item]
        return (xg if kind == "x" else pg).at[source, pl.ds(r0, n)]

    def move(item, source, to, send, recv):
        return pltpu.make_async_remote_copy(
            src_ref=part_of(item, source),
            dst_ref=part_of(item, source),
            send_sem=send.at[item],
            recv_sem=recv.at[item],
            device_id=(g, to),
            device_id_type=MESH,
        )

    def give(item):
        move(item, t, right, right_send, left_recv).start()
        move(item, t, left, left_send, right_recv).start()

    def hand_on(item):
        move(item, left, right, right_send, left_recv).wait_recv()
        if item in RELAY_RIGHT:
            move(item, left, right, hop_send, hop_recv).start()
        move(item, right, left, left_send, right_recv).wait_recv()
        if item not in RELAY_RIGHT:
            move(item, right, left, hop_send, hop_recv).start()

    def far_item(item):
        move(item, far, right, hop_send, hop_recv).wait_recv()

    for j in range(5):
        to_mate(j).start()

    dealt, by_slot = owner_tables(own_ref, spans_ref, adm_ref, perm_ref)
    by_req = dealt.T.astype(BF16)
    dealt = dealt.astype(BF16)
    long_own = fact(by_slot, 0, 2 * g) > 0.5
    sent = nt(dealt, p0_ref[...])
    wide_ref[...] = jnp.zeros_like(wide_ref)
    wide_ref[pl.ds(0, 64, stride=8), 0:16] = sent[0:64]
    wide_ref[pl.ds(1, 64, stride=8), 0:16] = sent[64:128]
    pbuf[...] = wide_ref[0:512, :].astype(BF16).reshape(64, 8, 128)
    pgot[g] = pbuf[g]

    to_mate(0).wait_recv()
    pg[t, 0:HALF, :] = jnp.where(long_own, part_ref[pl.ds(mine, HALF), :], pin[...])
    give(0)
    for j in range(4):
        to_mate(1 + j).wait_recv()
        rows = pl.ds(j * PIECE, PIECE)
        xg[t, rows, :] = jnp.where(long_own, xv_ref[pl.ds(mine + j * PIECE, PIECE), :], xin[rows, :])
        give(1 + j)
        if j == 0:
            scatter_rep(pbuf, pgot, p_send, p_recv, g, t)
    to_mate(5).start()
    to_mate(6).start()

    for c in range(8):
        rows = mm(dealt, km_ref[pl.ds(c, 128, stride=8), :].astype(BF16))
        wide_ref[pl.ds(c, 64, stride=16), :] = rows[0:64]
        wide_ref[pl.ds(8 + c, 64, stride=16), :] = rows[64:128]
    sbuf[...] = wide_ref[...].astype(BF16).reshape(64, 16, 128)
    sgot[g] = sbuf[g]
    scatter_rep(sbuf, sgot, st_send, st_recv, g, t)

    spread = (iota((128, WID), 1) // SPAN == iota((128, WID), 0)).astype(BF16)
    own_lane = iota((64, WID), 1) % SPAN == iota((64, WID), 0)
    row16 = iota((16, WID), 0)
    wait_rep(pgot, p_recv)
    wide_ref[0:512, :] = pgot[...].reshape(512, 128).astype(F32)
    before = []
    for s in range(2):
        vals = mm(wide_ref[pl.ds(s, 64, stride=8), :].astype(BF16), spread)
        before.append(jnp.sum(jnp.where(own_lane, vals, 0.0), axis=0, keepdims=True))
    final = x_ref[TAIL - 16 : TAIL, :].astype(F32)[15:16]
    firsts = [jnp.where(long_own, final, before[0]), before[1]]
    first_ref[...] = jnp.where(iota((8, WID), 0) == 0, firsts[0], firsts[1])
    cur = [x_ref[0:16, :].astype(F32), gx_ref[0:16, :].astype(F32), gx_ref[16:32, :].astype(F32)]
    ahead = [jnp.where(row16 == 0, f, pltpu.roll(x, 1, 0)) for x, f in zip(cur, before[:1] + firsts)]
    zsend[...] = mixed(cur[0], ahead[0], mc).astype(BF16)
    zpart[...] = mm(mixed(cur[0], ahead[0], mf).astype(BF16), sh_ref[...]).astype(BF16)
    to_mate(7).start()
    to_mate(8).start()
    for s in range(2):
        at = HALF + 16 * s
        xg[t, at : at + 16, :] = mixed(cur[1 + s], ahead[1 + s], mc).astype(BF16)
        pg[t, at : at + 16, :] = mm(mixed(cur[1 + s], ahead[1 + s], mf).astype(BF16), sh_ref[...]).astype(BF16)
    hand_on(0)
    hand_on(1)
    to_mate(7).wait_recv()
    to_mate(8).wait_recv()
    at = HALF + 32
    xg[t, at : at + 16, :] = jnp.where(long_own, zsend[...], zin[...])
    pg[t, at : at + 16, :] = jnp.where(long_own, zpart[...], zpin[...])
    for item in range(5, 8):
        give(item)

    def product(source, add):
        def tile(n, _):
            c = pl.ds(pl.multiple_of(n * 256, 256), 256)
            out = mm(xg[source], w_ref[pl.ds(pl.multiple_of(source * WID, WID), WID), c])
            acc[:, c] = acc[:, c] + out if add else out
            return 0

        lax.fori_loop(0, WID // 256, tile, 0)

    for k in range(TP):
        w_copy(k).wait()
    product(t, False)
    hand_on(2)

    counts = []
    wide_ref[0:512, :] = jnp.zeros((512, 128), F32)
    for s in range(2):
        count = fact(by_slot, 1, 2 * g + s).astype(jnp.int32)
        counts.append(count)
        rows = gx_ref[DRAFT * s : DRAFT * s + DRAFT, :].astype(F32)
        edge = jnp.sum(jnp.where(row16 == count - 1, rows, 0.0), axis=0, keepdims=True)
        edge = jnp.where(count > 0, edge, first_ref[s : s + 1, :])
        wide_ref[pl.ds(s, 64, stride=8), :] = nt(jnp.where(own_lane, edge, 0.0).astype(BF16), spread)
    ebuf[...] = wide_ref[0:512, :].astype(BF16).reshape(64, 8, 128)
    egot[g] = ebuf[g]
    hand_on(3)
    hand_on(4)

    wait_rep(sgot, st_recv)
    wide_ref[...] = sgot[...].reshape(1024, 128).astype(F32)
    for p in range(PAIRS):
        st0_ref[p] = wide_ref[pl.ds(p, 64, stride=16), :].astype(BF16)
    to_mate(11).start()

    for item in range(5, 8):
        hand_on(item)
    far_item(0)
    far_item(7)
    low = jnp.tanh(pg[0].astype(F32) + pg[1].astype(F32) + pg[2].astype(F32) + pg[3].astype(F32)).astype(BF16)
    lh[...] = low[0:HALF]
    ll_ref[...] = low[HALF:ROWS]
    swap = (iota((16, RANK), 0) == 0) & (core == 0)
    lh[0:16, :] = jnp.where(swap, ll_ref[32:33, :], lh[0:16, :])
    to_mate(9).start()
    lt_ref[pl.ds(mine, HALF), :] = lh[...]
    scatter_rep(ebuf, egot, e_send, e_recv, g, t)
    product(left, True)
    to_mate(5).wait_recv()
    to_mate(6).wait_recv()
    to_mate(9).wait_recv()

    same = iota((128, 128), 0) // SPAN == iota((128, 128), 1) // SPAN
    heads_sum = same.astype(BF16)
    anchor, boost, scale, shift = anchor_ref[...], boost_ref[...], scale_ref[...], shift_ref[...]

    def ready(i, _):
        rows = pl.ds(pl.multiple_of(i * CHUNK, 16), CHUNK)
        log = -jnp.exp(anchor_ref[:, cols] + mm(lt_ref[rows, :], ex_ref[:, cols]))
        r = jnp.where(long_own, rown[rows, :], rmate[rows, :]).astype(F32)
        k = jnp.where(long_own, kown[rows, :], kmate[rows, :]).astype(F32)
        incl = running(log, CHUNK)
        q, kk, ri = scaled(r, k, incl, log, CHUNK)
        ri_ref[rows, :] = ri
        last = incl[CHUNK - 1 : CHUNK]
        kd = k * jnp.exp(last - incl)
        keep = jnp.exp(last)
        gain = mm(stack((r * boost_ref[:, cols] * k).astype(BF16), SPLIT), heads_sum)
        for p in range(SPLIT):
            c = lanes(p)
            gain_ref[rows, c] = gain[CHUNK * p : CHUNK * p + CHUNK]
            sc_ref[SPLIT * i + p] = scored(q[:, c], kk[:, c], CHUNK)
            kd_ref[SPLIT * i + p] = kd[:, c].T.astype(BF16)
            keep_ref[SPLIT * i + p] = column(keep[:, c])
        return 0

    lax.fori_loop(0, STEPS, ready, 0)
    product(right, True)
    for item in range(1, 7):
        far_item(item)
    product(far, True)
    vh[...] = acc[0:HALF, :].astype(BF16)
    vl_ref[...] = acc[HALF:ROWS, :].astype(BF16)
    vh[0:16, :] = jnp.where((row16 == 0) & (core == 0), vl_ref[32:33, :], vh[0:16, :])
    to_mate(10).start()
    vt_ref[pl.ds(mine, HALF), :] = vh[:, cols]

    for s in range(2):
        rows = slice(DRAFT * s, DRAFT * s + DRAFT)
        log = -jnp.exp(anchor + mm(ll_ref[rows, :], ex_ref[...]))
        r, k, v = gr_ref[rows, :].astype(F32), gk_ref[rows, :].astype(F32), vl_ref[rows, :]
        incl = running(log, DRAFT)
        q, kk, ri = scaled(r, k, incl, log, DRAFT)
        dri_ref[rows, :] = ri
        gain = mm(stack((r * boost * k).astype(BF16), PAIRS), heads_sum)
        taken = row16 < counts[s]
        upto = jnp.sum(jnp.where(taken, log, 0.0), axis=0, keepdims=True)
        weight = jnp.where(taken, jnp.exp(jnp.where(taken, upto - incl, 0.0)), 0.0)
        kd = (k * weight).astype(BF16)
        keep = jnp.exp(upto)
        low16 = iota((DRAFT, 128), 1) < SPAN
        for p in range(PAIRS):
            c = lanes(p)
            both = mm(scored(q[:, c], kk[:, c], DRAFT), v[:, c])
            inner = jnp.where(low16, both[0:DRAFT], both[DRAFT : 2 * DRAFT])
            dy_ref[s, DRAFT * p : DRAFT * p + DRAFT, :] = (
                inner + gain[DRAFT * p : DRAFT * p + DRAFT] * v[:, c].astype(F32)
            )
            du_ref[s, p] = jnp.where(same, tn(kd[:, c], v[:, c]), 0.0)
            dk_ref[s, p] = column(keep[:, c])

    def drafted(s, states):
        rows = slice(DRAFT * s, DRAFT * s + DRAFT)
        y = dy_ref[s] + jnp.concatenate(
            [mm(dri_ref[rows, lanes(p)], states[p].astype(BF16)) for p in range(PAIRS)], axis=0
        )
        for p in range(PAIRS):
            end = states[p] * dk_ref[s, p] + du_ref[s, p]
            wide_ref[pl.ds(512 * s + p, 64, stride=8), :] = end[0:64] + end[64:128]
        rbuf[s] = wide_ref[512 * s : 512 * s + 512, :].astype(BF16).reshape(64, 8, 128)
        rgot[s, g] = rbuf[s, g]
        scatter_rep(rbuf.at[s], rgot.at[s], b_send.at[s], b_recv.at[s], g, t)
        draft_ref[rows, :] = normed(y, heads_sum, scale, shift, DRAFT, PAIRS).astype(BF16)

    late_states = [halves(wide_ref[pl.ds(8 + p, 64, stride=16), :]) for p in range(PAIRS)]
    for p in range(PAIRS):
        dk_ref[2, p] = late_states[p]
    drafted(1, [dk_ref[2, p] for p in range(PAIRS)])

    to_mate(11).wait_recv()
    for p in range(SPLIT):
        start = jnp.where(long_own, st0_ref[core * SPLIT + p], stm_ref[p])
        st_ref[p] = halves(start.astype(F32))
    to_mate(10).wait_recv()
    low32 = iota((CHUNK, 128), 1) < SPAN

    def step(i, _):
        rows = pl.ds(pl.multiple_of(i * CHUNK, 16), CHUNK)
        for p in range(SPLIT):
            c = lanes(p)
            v = vt_ref[rows, c]
            both = mm(sc_ref[SPLIT * i + p], v)
            state = st_ref[p]
            y = jnp.where(low32, both[0:CHUNK], both[CHUNK : 2 * CHUNK])
            y_ref[rows, c] = y + mm(ri_ref[rows, c], state.astype(BF16)) + gain_ref[rows, c] * v.astype(F32)
            st_ref[p] = state * keep_ref[SPLIT * i + p] + jnp.where(same, mm(kd_ref[SPLIT * i + p], v), 0.0)
        return 0

    lax.fori_loop(0, STEPS, step, 0, unroll=3)
    to_mate(12).start()

    to_mate(12).wait_recv()
    states = []
    for p in range(PAIRS):
        here = core == p // SPLIT
        end = jnp.where(here, st_ref[p % SPLIT], endm_ref[p % SPLIT])
        states.append(jnp.where(long_own, end, halves(st0_ref[p].astype(F32))))
    for p in range(PAIRS):
        dk_ref[2, p] = states[p]
    drafted(0, [dk_ref[2, p] for p in range(PAIRS)])

    def finish(i, _):
        rows = pl.ds(pl.multiple_of(i * CHUNK, 16), CHUNK)
        y = stack(y_ref[rows, :], SPLIT)
        o_ref[rows, :] = normed(y, heads_sum, scale_ref[:, cols], shift_ref[:, cols], CHUNK, SPLIT).astype(BF16)
        return 0

    lax.fori_loop(0, STEPS, finish, 0)
    to_mate(13).start()
    tail_ref[:, cols] = jnp.where(long_own, o_ref[...], jnp.zeros((TAIL, SIDE), BF16))

    wait_rep(egot, e_recv)
    wide_ref[0:512, :] = egot[...].reshape(512, 128).astype(F32)
    edges = jnp.concatenate([wide_ref[pl.ds(0, 64, stride=8), :], wide_ref[pl.ds(1, 64, stride=8), :]], axis=0)
    prior_ref[...] = tn(edges.astype(BF16), dealt)[0:16].astype(BF16)
    to_mate(13).wait_recv()
    tail_ref[:, mate_cols] = jnp.where(long_own, om_ref[...], jnp.zeros((TAIL, SIDE), BF16))
    for s in range(2):
        wait_rep(rgot.at[s], b_recv.at[s])
    wide_ref[...] = rgot[...].reshape(1024, 128).astype(F32)
    for c in range(8):
        rows = jnp.concatenate(
            [wide_ref[pl.ds(c, 64, stride=8), :], wide_ref[pl.ds(512 + c, 64, stride=8), :]], axis=0
        )
        state_ref[pl.ds(c, 128, stride=8), :] = mm(by_req, rows.astype(BF16))

    wait_rep(pbuf, p_send)
    wait_rep(sbuf, st_send)
    wait_rep(ebuf, e_send)
    for s in range(2):
        wait_rep(rbuf.at[s], b_send.at[s])
    for j in range(14):
        to_mate(j).wait_send()
    for item in range(8):
        move(item, t, right, right_send, left_recv).wait_send()
        move(item, t, left, left_send, right_recv).wait_send()
        move(item, far, right, hop_send, hop_recv).wait_send()


def place_kernel(a_ref, b_ref, c_ref, d_ref, a_out, b_out, c_out, d_out, sem):
    pairs = ((a_ref, a_out), (b_ref, b_out), (c_ref, c_out), (d_ref, d_out))
    copies = [pltpu.make_async_copy(src, dst, sem.at[i]) for i, (src, dst) in enumerate(pairs)]
    for c in copies:
        c.start()
    for c in copies:
        c.wait()


VM = pl.BlockSpec(memory_space=pltpu.VMEM)
ANY = pl.BlockSpec(memory_space=pl.ANY)
DMA = pltpu.SemaphoreType.DMA


def local(
    suffix_source, suffix_accept, suffix_address, guess_lane_source, guess_lane_accept, guess_lane_address,
    content_map, forget_shrink_map, forget_expand_map, forget_lane_anchor, present_boost,
    content_blend_share, forget_blend_share, lane_normal_scale, lane_normal_shift,
    kernel_memory_saved, prior_source_saved, lane_owner, request_spans, admitted_guesses,
):
    small = [a.reshape(1, 128) for a in (lane_owner, request_spans, admitted_guesses)]
    chan = [
        a.reshape(1, WID)
        for a in (forget_lane_anchor, present_boost, lane_normal_scale, lane_normal_shift)
    ]
    sds = jax.ShapeDtypeStruct
    shapes = (
        sds((TAIL, WID), BF16),
        sds((2 * DRAFT, WID), BF16),
        sds((1024, 128), F32),
        sds((16, 128), BF16),
    )
    vm = pltpu.VMEM
    row, ints, drafts = vm((1, WID), F32), vm((1, 128), jnp.int32), vm((2 * DRAFT, WID), BF16)
    side, tile16, tile8 = vm((TAIL, SIDE), BF16), vm((REP, 16, 128), BF16), vm((REP, 8, 128), BF16)
    outs = pl.pallas_call(
        mix_kernel,
        name="time_mix",
        out_shape=shapes,
        in_specs=[ANY] * 20,
        out_specs=(VM,) * 4,
        scratch_shapes=[
            vm((TAIL, WID), BF16), drafts, vm((1024, 128), F32), vm((16, 128), BF16), row, row,
            ints, ints, ints, drafts, drafts, vm((RANK, WID), BF16), row, row, row, row,
            vm((TP * WID, WID), BF16), vm((WID, RANK), BF16), side, side,
            vm((128, 128), F32), vm((1024, 128), F32), tile16, tile16, tile8, tile8,
            vm((TAIL, WID), BF16), vm((TAIL, RANK), BF16), vm((HALF, WID), BF16), vm((HALF, RANK), BF16),
            vm((16, WID), BF16), vm((16, RANK), BF16), vm((16, WID), BF16), vm((16, RANK), BF16),
            vm((TP, ROWS, WID), BF16), vm((TP, ROWS, RANK), BF16), vm((ROWS, WID), F32),
            vm((HALF, WID), BF16), vm((HALF, RANK), BF16), vm((LATE, WID), BF16), vm((LATE, RANK), BF16),
            vm((8, WID), F32), side, vm((TAIL, RANK), BF16), side, side,
            vm((PAIRS, 64, 128), BF16), vm((SPLIT, 64, 128), BF16),
            vm((STEPS * SPLIT, 2 * CHUNK, CHUNK), BF16), side, vm((TAIL, SIDE), F32),
            vm((STEPS * SPLIT, 128, CHUNK), BF16), vm((STEPS * SPLIT, 128, 128), F32),
            vm((SPLIT, 128, 128), F32), vm((SPLIT, 128, 128), F32), vm((TAIL, SIDE), F32), side, side,
            vm((2, 128, 128), F32), drafts, vm((2, PAIRS, 128, 128), F32), vm((3, PAIRS, 128, 128), F32),
            vm((2, REP, 8, 128), BF16), vm((2, REP, 8, 128), BF16), tile8, tile8,
            DMA((19,)), DMA((TP,)), DMA, DMA, DMA, DMA, DMA, DMA, DMA((2,)), DMA((2,)), DMA((14,)), DMA((14,)),
            DMA((8,)), DMA((8,)), DMA((8,)), DMA((8,)), DMA((8,)), DMA((8,)),
        ],
        compiler_params=pltpu.CompilerParams(
            collective_id=0, has_side_effects=True, vmem_limit_bytes=56 << 20
        ),
    )(
        suffix_source.reshape(TAIL, WID),
        guess_lane_source.reshape(2 * DRAFT, WID),
        kernel_memory_saved.reshape(1024, 128),
        prior_source_saved.reshape(128, 16).T,
        content_blend_share.reshape(1, WID),
        forget_blend_share.reshape(1, WID),
        *small,
        guess_lane_accept.reshape(2 * DRAFT, WID),
        guess_lane_address.reshape(2 * DRAFT, WID),
        forget_expand_map,
        *chan,
        content_map,
        forget_shrink_map,
        suffix_accept.reshape(TAIL, WID),
        suffix_address.reshape(TAIL, WID),
    )
    tail, draft, state, prior = pl.pallas_call(
        place_kernel,
        name="place",
        out_shape=shapes,
        in_specs=[VM] * 4,
        out_specs=(ANY,) * 4,
        scratch_shapes=[DMA((4,))],
    )(*outs)
    return (
        tail.reshape(1, TAIL, WID),
        draft.reshape(2, DRAFT, WID),
        state.reshape(128, 1, WID),
        prior.T.reshape(128, 1, 16),
    )


def solution(mesh):
    rows, cols, chan = P("rep", None, "tp"), P(None, "tp"), P("tp")
    cache = P(None, "rep", "tp")
    return jax.shard_map(
        local,
        mesh=mesh,
        in_specs=(rows,) * 6 + (cols, P(), cols) + (chan,) * 6 + (cache, cache, P(), P(), P()),
        out_specs=(rows, rows, cache, cache),
        check_vma=False,
    )
```

time: 87.8 us -> 63.9 us (0.73)
  Pallas kernels: 75.5 us -> 63.1 us
  local copies, waits for them, and re-layouts: 11.2 us -> 0 us
    pallas_call x2, Pallas kernels: 75.5 us -> 63.1 us  [the longest x1 60.7 us: local(): pl.pallas_call(mix_kernel, name='time_mix', out_shape=shapes, in_specs=[A...]
    unnamed x42 -> x0, local copies, waits for them, and re-layouts: 11.2 us -> none
where the time goes in v2:
time: 63.9 us; the launch traced here: 63.8 us
  Pallas kernels  63.1 us (99%)
  between operations  0.65 us (1%)
    pallas_call x1, Pallas kernels, local(): pl.pallas_call(mix_kernel, name='time_mix', out_shape=shapes, in_specs=[A...  60.7 us
    pallas_call x1, Pallas kernels, local(): pl.pallas_call(place_kernel, name='place', out_shape=shapes, in_specs=[VM...  2.43 us

profile of v2, /device:TPU:1, one launch (start us, length us, event | category | flops | bytes accessed | tf_op | source)
XLA Modules:
  0.0 63.8 jit_solution(4264896449937145626)
XLA Ops:
  0.6 60.7 %time_mix.1 = (bf16[384,1024]{1,0:T(8,128)(2,1)}, bf16[32,1024]{1,0:T(8,128)(2,1)}, f32[1024,128]{1,0:T(8,128)}, bf16[16,128]{1,0:T(8,128)(2,1)}) custom-call(bf16[384,1024]{1,0:T(8,128)(2,1)} %bitcast.25, bf16[32,1024]{1,0:T(8,128)(2,1)} %bitcast.29, f32[1024,128]{1,0:T(8,128)} %bitcast.28, bf16[16,128]{1,0:T(8,128)(2,1)} %bitcast.32, f32[1,1024]{1,0:T(1,128)} %bitcast.33, ...), custom_call_target="tpu_custom_call" | custom-call | tf_op jit(solution)/shard_map/time_mix/pallas_call | solution.py:583
  61.3 2.4 %place.1 = (bf16[384,1024]{1,0:T(8,128)(2,1)}, bf16[32,1024]{1,0:T(8,128)(2,1)}, f32[1024,128]{1,0:T(8,128)}, bf16[16,128]{1,0:T(8,128)(2,1)}) custom-call(bf16[384,1024]{1,0:T(8,128)(2,1)} %get-tuple-element.12.a_ref, bf16[32,1024]{1,0:T(8,128)(2,1)} %get-tuple-element.13.b_ref, f32[1024,128]{1,0:T(8,128)} %get-tuple-element.14.c_ref, ...), custom_call_target="tpu_custom_call" | custom-call | tf_op jit(solution)/shard_map/place/pallas_call | solution.py:628

commit v3 on v2

--- a/solution.py
+++ b/solution.py
@@ -9,6 +9,7 @@
 DRAFT = 16
 EPS = 0.00064
 REP = 64
+ROW = 8
 TP = 4
 WID = 1024
 TAIL = 384
@@ -37,7 +38,8 @@
     ("x", 208, 32),
     ("p", 192, 48),
 )
-RELAY_RIGHT = (0, 1, 3, 5, 7)
+RELAY_RIGHT = (1, 3, 5)
+DIRECT = (0, 7)
 
 
 def iota(shape, dim):
@@ -73,12 +75,18 @@
     return jnp.sum(jnp.sum(here, axis=1, keepdims=True), axis=0, keepdims=True)
 
 
-def greet_rep(barrier, g, t):
-    def one(d, _):
-        pl.semaphore_signal(barrier, inc=1, device_id=(lax.rem(g + d, REP), t), device_id_type=MESH)
-        return 0
-
-    lax.fori_loop(1, REP, one, 0)
+def greet_near(barrier, g, t):
+    near = [(g, lax.rem(t + d, TP)) for d in range(1, TP)]
+    near += [(g - lax.rem(g, ROW) + lax.rem(g + d, ROW), t) for d in range(1, ROW)]
+    near += [(lax.rem(g + ROW * d, REP), t) for d in (1, 2, 6, 7)]
+    for to in near:
+        pl.semaphore_signal(barrier, inc=1, device_id=to, device_id_type=MESH)
+    return len(near)
+
+
+def pass_on(sem, g, t, steps):
+    for d in steps:
+        pl.semaphore_signal(sem, inc=1, device_id=(lax.rem(g + ROW * d, REP), t), device_id_type=MESH)
 
 
 def scatter_rep(src, dst, send, recv, g, t):
@@ -94,7 +102,7 @@
         ).start()
         return 0
 
-    lax.fori_loop(1, REP, one, 0)
+    lax.fori_loop(1, REP, one, 0, unroll=7)
 
 
 def wait_rep(buf, sem):
@@ -168,11 +176,11 @@
     x_ref, gx_ref, km_ref, p0_ref, mc_ref, mf_ref, own_ref, spans_ref, adm_ref, gr_ref, gk_ref, ex_ref,
     anchor_ref, boost_ref, scale_ref, shift_ref, w_ref, sh_ref, rown, kown,
     perm_ref, wide_ref, sbuf, sgot, pbuf, pgot, xv_ref, part_ref, xin, pin, zsend, zpart, zin, zpin,
-    xg, pg, acc, vh, lh, vl_ref, ll_ref, first_ref, vt_ref, lt_ref, rmate, kmate, st0_ref, stm_ref,
+    xg, pg, acc, vh, lh, vl_ref, ll_ref, vt_ref, lt_ref, rmate, kmate, st0_ref, stm_ref,
     sc_ref, ri_ref, gain_ref, kd_ref, keep_ref, st_ref, endm_ref, y_ref, o_ref, om_ref,
-    dy_ref, dri_ref, du_ref, dk_ref, rbuf, rgot, ebuf, egot,
+    dy_ref, dri_ref, du_ref, dk_ref, rbuf, rgot, ebuf, egot, lz_ref,
     in_sem, w_sem, st_send, st_recv, p_send, p_recv, e_send, e_recv, b_send, b_recv, mate_send, mate_recv,
-    right_send, left_recv, left_send, right_recv, hop_send, hop_recv,
+    right_send, left_recv, left_send, right_recv, hop_send, hop_recv, round1, round2,
 ):
     g, t = lax.axis_index("rep"), lax.axis_index("tp")
     core = lax.rem(g, 2)
@@ -204,9 +212,7 @@
         w_copy(k).start()
 
     barrier = pltpu.get_barrier_semaphore()
-    greet_rep(barrier, g, t)
-    for d in range(1, TP):
-        pl.semaphore_signal(barrier, inc=1, device_id=(g, lax.rem(t + d, TP)), device_id_type=MESH)
+    greeted = greet_near(barrier, g, t)
 
     for i in range(4):
         in_copy(i).wait()
@@ -224,7 +230,8 @@
     lax.fori_loop(0, TAIL // PIECE, mix_rows, 0)
     for i in range(4, len(plain)):
         in_copy(i).wait()
-    pl.semaphore_wait(barrier, REP - 1 + TP - 1)
+    pl.semaphore_wait(barrier, greeted)
+    pass_on(round1, g, t, (1, 2, 6, 7))
 
     moves = {
         0: (part_ref.at[pl.ds(other, HALF)], pin),
@@ -237,6 +244,7 @@
         11: (st0_ref.at[pl.ds((1 - core) * SPLIT, SPLIT)], stm_ref),
         12: (st_ref, endm_ref),
         13: (o_ref, om_ref),
+        14: (ll_ref.at[pl.ds(32, 16)], lz_ref),
     }
     for j in range(4):
         moves[1 + j] = (xv_ref.at[pl.ds(other + j * PIECE, PIECE)], xin.at[pl.ds(j * PIECE, PIECE)])
@@ -268,13 +276,15 @@
     def give(item):
         move(item, t, right, right_send, left_recv).start()
         move(item, t, left, left_send, right_recv).start()
+        if item in DIRECT:
+            move(item, t, far, hop_send, hop_recv).start()
 
     def hand_on(item):
         move(item, left, right, right_send, left_recv).wait_recv()
         if item in RELAY_RIGHT:
             move(item, left, right, hop_send, hop_recv).start()
         move(item, right, left, left_send, right_recv).wait_recv()
-        if item not in RELAY_RIGHT:
+        if item not in RELAY_RIGHT + DIRECT:
             move(item, right, left, hop_send, hop_recv).start()
 
     def far_item(item):
@@ -302,10 +312,25 @@
         rows = pl.ds(j * PIECE, PIECE)
         xg[t, rows, :] = jnp.where(long_own, xv_ref[pl.ds(mine + j * PIECE, PIECE), :], xin[rows, :])
         give(1 + j)
-        if j == 0:
-            scatter_rep(pbuf, pgot, p_send, p_recv, g, t)
+        if j == 1:
+            pl.semaphore_wait(round1, 4)
+            pass_on(round2, g, t, (3, 4, 5))
     to_mate(5).start()
     to_mate(6).start()
+
+    hand_on(0)
+    far_item(0)
+
+    def low_rank(r0, n):
+        parts = [pg[k, r0 : r0 + n, :].astype(F32) for k in range(TP)]
+        return jnp.tanh(parts[0] + parts[1] + parts[2] + parts[3]).astype(BF16)
+
+    lh[...] = low_rank(0, HALF)
+    to_mate(9).start()
+    lt_ref[pl.ds(mine, HALF), :] = lh[...]
+    pl.semaphore_wait(round2, 3)
+    scatter_rep(pbuf, pgot, p_send, p_recv, g, t)
+    hand_on(1)
 
     for c in range(8):
         rows = mm(dealt, km_ref[pl.ds(c, 128, stride=8), :].astype(BF16))
@@ -314,89 +339,7 @@
     sbuf[...] = wide_ref[...].astype(BF16).reshape(64, 16, 128)
     sgot[g] = sbuf[g]
     scatter_rep(sbuf, sgot, st_send, st_recv, g, t)
-
-    spread = (iota((128, WID), 1) // SPAN == iota((128, WID), 0)).astype(BF16)
-    own_lane = iota((64, WID), 1) % SPAN == iota((64, WID), 0)
-    row16 = iota((16, WID), 0)
-    wait_rep(pgot, p_recv)
-    wide_ref[0:512, :] = pgot[...].reshape(512, 128).astype(F32)
-    before = []
-    for s in range(2):
-        vals = mm(wide_ref[pl.ds(s, 64, stride=8), :].astype(BF16), spread)
-        before.append(jnp.sum(jnp.where(own_lane, vals, 0.0), axis=0, keepdims=True))
-    final = x_ref[TAIL - 16 : TAIL, :].astype(F32)[15:16]
-    firsts = [jnp.where(long_own, final, before[0]), before[1]]
-    first_ref[...] = jnp.where(iota((8, WID), 0) == 0, firsts[0], firsts[1])
-    cur = [x_ref[0:16, :].astype(F32), gx_ref[0:16, :].astype(F32), gx_ref[16:32, :].astype(F32)]
-    ahead = [jnp.where(row16 == 0, f, pltpu.roll(x, 1, 0)) for x, f in zip(cur, before[:1] + firsts)]
-    zsend[...] = mixed(cur[0], ahead[0], mc).astype(BF16)
-    zpart[...] = mm(mixed(cur[0], ahead[0], mf).astype(BF16), sh_ref[...]).astype(BF16)
-    to_mate(7).start()
-    to_mate(8).start()
-    for s in range(2):
-        at = HALF + 16 * s
-        xg[t, at : at + 16, :] = mixed(cur[1 + s], ahead[1 + s], mc).astype(BF16)
-        pg[t, at : at + 16, :] = mm(mixed(cur[1 + s], ahead[1 + s], mf).astype(BF16), sh_ref[...]).astype(BF16)
-    hand_on(0)
-    hand_on(1)
-    to_mate(7).wait_recv()
-    to_mate(8).wait_recv()
-    at = HALF + 32
-    xg[t, at : at + 16, :] = jnp.where(long_own, zsend[...], zin[...])
-    pg[t, at : at + 16, :] = jnp.where(long_own, zpart[...], zpin[...])
-    for item in range(5, 8):
-        give(item)
-
-    def product(source, add):
-        def tile(n, _):
-            c = pl.ds(pl.multiple_of(n * 256, 256), 256)
-            out = mm(xg[source], w_ref[pl.ds(pl.multiple_of(source * WID, WID), WID), c])
-            acc[:, c] = acc[:, c] + out if add else out
-            return 0
-
-        lax.fori_loop(0, WID // 256, tile, 0)
-
-    for k in range(TP):
-        w_copy(k).wait()
-    product(t, False)
     hand_on(2)
-
-    counts = []
-    wide_ref[0:512, :] = jnp.zeros((512, 128), F32)
-    for s in range(2):
-        count = fact(by_slot, 1, 2 * g + s).astype(jnp.int32)
-        counts.append(count)
-        rows = gx_ref[DRAFT * s : DRAFT * s + DRAFT, :].astype(F32)
-        edge = jnp.sum(jnp.where(row16 == count - 1, rows, 0.0), axis=0, keepdims=True)
-        edge = jnp.where(count > 0, edge, first_ref[s : s + 1, :])
-        wide_ref[pl.ds(s, 64, stride=8), :] = nt(jnp.where(own_lane, edge, 0.0).astype(BF16), spread)
-    ebuf[...] = wide_ref[0:512, :].astype(BF16).reshape(64, 8, 128)
-    egot[g] = ebuf[g]
-    hand_on(3)
-    hand_on(4)
-
-    wait_rep(sgot, st_recv)
-    wide_ref[...] = sgot[...].reshape(1024, 128).astype(F32)
-    for p in range(PAIRS):
-        st0_ref[p] = wide_ref[pl.ds(p, 64, stride=16), :].astype(BF16)
-    to_mate(11).start()
-
-    for item in range(5, 8):
-        hand_on(item)
-    far_item(0)
-    far_item(7)
-    low = jnp.tanh(pg[0].astype(F32) + pg[1].astype(F32) + pg[2].astype(F32) + pg[3].astype(F32)).astype(BF16)
-    lh[...] = low[0:HALF]
-    ll_ref[...] = low[HALF:ROWS]
-    swap = (iota((16, RANK), 0) == 0) & (core == 0)
-    lh[0:16, :] = jnp.where(swap, ll_ref[32:33, :], lh[0:16, :])
-    to_mate(9).start()
-    lt_ref[pl.ds(mine, HALF), :] = lh[...]
-    scatter_rep(ebuf, egot, e_send, e_recv, g, t)
-    product(left, True)
-    to_mate(5).wait_recv()
-    to_mate(6).wait_recv()
-    to_mate(9).wait_recv()
 
     same = iota((128, 128), 0) // SPAN == iota((128, 128), 1) // SPAN
     heads_sum = same.astype(BF16)
@@ -422,8 +365,102 @@
             keep_ref[SPLIT * i + p] = column(keep[:, c])
         return 0
 
-    lax.fori_loop(0, STEPS, ready, 0)
+    def product(source, add):
+        def tile(n, _):
+            c = pl.ds(pl.multiple_of(n * 256, 256), 256)
+            out = mm(xg[source], w_ref[pl.ds(pl.multiple_of(source * WID, WID), WID), c])
+            acc[:, c] = acc[:, c] + out if add else out
+            return 0
+
+        lax.fori_loop(0, WID // 256, tile, 0)
+
+    to_mate(5).wait_recv()
+    to_mate(6).wait_recv()
+    to_mate(9).wait_recv()
+
+    spread = (iota((128, WID), 1) // SPAN == iota((128, WID), 0)).astype(BF16)
+    own_lane = iota((64, WID), 1) % SPAN == iota((64, WID), 0)
+    row16 = iota((16, WID), 0)
+    firsts = []
+
+    def late_rows():
+        wait_rep(pgot, p_recv)
+        wide_ref[0:512, :] = pgot[...].reshape(512, 128).astype(F32)
+        before = []
+        for s in range(2):
+            vals = mm(wide_ref[pl.ds(s, 64, stride=8), :].astype(BF16), spread)
+            before.append(jnp.sum(jnp.where(own_lane, vals, 0.0), axis=0, keepdims=True))
+        final = x_ref[TAIL - 16 : TAIL, :].astype(F32)[15:16]
+        firsts.extend([jnp.where(long_own, final, before[0]), before[1]])
+        cur = [x_ref[0:16, :].astype(F32), gx_ref[0:16, :].astype(F32), gx_ref[16:32, :].astype(F32)]
+        ahead = [jnp.where(row16 == 0, f, pltpu.roll(x, 1, 0)) for x, f in zip(cur, before[:1] + firsts)]
+        zsend[...] = mixed(cur[0], ahead[0], mc).astype(BF16)
+        zpart[...] = mm(mixed(cur[0], ahead[0], mf).astype(BF16), sh_ref[...]).astype(BF16)
+        to_mate(7).start()
+        to_mate(8).start()
+        for s in range(2):
+            at = HALF + 16 * s
+            xg[t, at : at + 16, :] = mixed(cur[1 + s], ahead[1 + s], mc).astype(BF16)
+            pg[t, at : at + 16, :] = mm(mixed(cur[1 + s], ahead[1 + s], mf).astype(BF16), sh_ref[...]).astype(BF16)
+
+    def give_late():
+        to_mate(7).wait_recv()
+        to_mate(8).wait_recv()
+        at = HALF + 32
+        xg[t, at : at + 16, :] = jnp.where(long_own, zsend[...], zin[...])
+        pg[t, at : at + 16, :] = jnp.where(long_own, zpart[...], zpin[...])
+        for item in (7, 5, 6):
+            give(item)
+
+    counts = []
+
+    def edges_out():
+        wide_ref[0:512, :] = jnp.zeros((512, 128), F32)
+        for s in range(2):
+            count = fact(by_slot, 1, 2 * g + s).astype(jnp.int32)
+            counts.append(count)
+            rows = gx_ref[DRAFT * s : DRAFT * s + DRAFT, :].astype(F32)
+            edge = jnp.sum(jnp.where(row16 == count - 1, rows, 0.0), axis=0, keepdims=True)
+            edge = jnp.where(count > 0, edge, firsts[s])
+            wide_ref[pl.ds(s, 64, stride=8), :] = nt(jnp.where(own_lane, edge, 0.0).astype(BF16), spread)
+        ebuf[...] = wide_ref[0:512, :].astype(BF16).reshape(64, 8, 128)
+        egot[g] = ebuf[g]
+        scatter_rep(ebuf, egot, e_send, e_recv, g, t)
+
+    lax.fori_loop(1, 4, ready, 0)
+    hand_on(3)
+    late_rows()
+    hand_on(4)
+    lax.fori_loop(4, 6, ready, 0)
+    give_late()
+    edges_out()
+    wait_rep(sgot, st_recv)
+    wide_ref[...] = sgot[...].reshape(1024, 128).astype(F32)
+    for p in range(PAIRS):
+        st0_ref[p] = wide_ref[pl.ds(p, 64, stride=16), :].astype(BF16)
+    to_mate(11).start()
+    for p in range(PAIRS):
+        dk_ref[2, p] = halves(wide_ref[pl.ds(8 + p, 64, stride=16), :])
+    lax.fori_loop(6, STEPS, ready, 0)
+    for k in range(TP):
+        w_copy(k).wait()
+    hand_on(7)
+    far_item(7)
+    hand_on(5)
+    hand_on(6)
+    ll_ref[...] = low_rank(HALF, LATE)
+    to_mate(14).start()
+    product(t, False)
+    product(left, True)
+    to_mate(14).wait_recv()
+    head = jnp.where(core == 0, ll_ref[32:33, :], lz_ref[0:1, :])
+    lt_ref[0:16, :] = jnp.where(iota((16, RANK), 0) == 0, head, lt_ref[0:16, :])
+    ready(0, 0)
     product(right, True)
+    to_mate(11).wait_recv()
+    for p in range(SPLIT):
+        start = jnp.where(long_own, st0_ref[core * SPLIT + p], stm_ref[p])
+        st_ref[p] = halves(start.astype(F32))
     for item in range(1, 7):
         far_item(item)
     product(far, True)
@@ -433,7 +470,9 @@
     to_mate(10).start()
     vt_ref[pl.ds(mine, HALF), :] = vh[:, cols]
 
-    for s in range(2):
+    low16 = iota((DRAFT, 128), 1) < SPAN
+
+    def draft_ready(s):
         rows = slice(DRAFT * s, DRAFT * s + DRAFT)
         log = -jnp.exp(anchor + mm(ll_ref[rows, :], ex_ref[...]))
         r, k, v = gr_ref[rows, :].astype(F32), gk_ref[rows, :].astype(F32), vl_ref[rows, :]
@@ -446,7 +485,6 @@
         weight = jnp.where(taken, jnp.exp(jnp.where(taken, upto - incl, 0.0)), 0.0)
         kd = (k * weight).astype(BF16)
         keep = jnp.exp(upto)
-        low16 = iota((DRAFT, 128), 1) < SPAN
         for p in range(PAIRS):
             c = lanes(p)
             both = mm(scored(q[:, c], kk[:, c], DRAFT), v[:, c])
@@ -457,28 +495,15 @@
             du_ref[s, p] = jnp.where(same, tn(kd[:, c], v[:, c]), 0.0)
             dk_ref[s, p] = column(keep[:, c])
 
-    def drafted(s, states):
+    def accept(s, p, state):
         rows = slice(DRAFT * s, DRAFT * s + DRAFT)
-        y = dy_ref[s] + jnp.concatenate(
-            [mm(dri_ref[rows, lanes(p)], states[p].astype(BF16)) for p in range(PAIRS)], axis=0
-        )
-        for p in range(PAIRS):
-            end = states[p] * dk_ref[s, p] + du_ref[s, p]
-            wide_ref[pl.ds(512 * s + p, 64, stride=8), :] = end[0:64] + end[64:128]
-        rbuf[s] = wide_ref[512 * s : 512 * s + 512, :].astype(BF16).reshape(64, 8, 128)
-        rgot[s, g] = rbuf[s, g]
-        scatter_rep(rbuf.at[s], rgot.at[s], b_send.at[s], b_recv.at[s], g, t)
-        draft_ref[rows, :] = normed(y, heads_sum, scale, shift, DRAFT, PAIRS).astype(BF16)
-
-    late_states = [halves(wide_ref[pl.ds(8 + p, 64, stride=16), :]) for p in range(PAIRS)]
-    for p in range(PAIRS):
-        dk_ref[2, p] = late_states[p]
-    drafted(1, [dk_ref[2, p] for p in range(PAIRS)])
-
-    to_mate(11).wait_recv()
-    for p in range(SPLIT):
-        start = jnp.where(long_own, st0_ref[core * SPLIT + p], stm_ref[p])
-        st_ref[p] = halves(start.astype(F32))
+        at = slice(DRAFT * p, DRAFT * p + DRAFT)
+        dy_ref[s, at, :] = dy_ref[s, at, :] + mm(dri_ref[rows, lanes(p)], state.astype(BF16))
+        end = state * dk_ref[s, p] + du_ref[s, p]
+        wide_ref[pl.ds(8 * s + p, 64, stride=16), :] = end[0:64] + end[64:128]
+
+    draft_ready(0)
+
     to_mate(10).wait_recv()
     low32 = iota((CHUNK, 128), 1) < SPAN
 
@@ -497,15 +522,20 @@
     lax.fori_loop(0, STEPS, step, 0, unroll=3)
     to_mate(12).start()
 
+    draft_ready(1)
+    for p in range(PAIRS):
+        accept(1, p, dk_ref[2, p])
     to_mate(12).wait_recv()
-    states = []
     for p in range(PAIRS):
-        here = core == p // SPLIT
-        end = jnp.where(here, st_ref[p % SPLIT], endm_ref[p % SPLIT])
-        states.append(jnp.where(long_own, end, halves(st0_ref[p].astype(F32))))
-    for p in range(PAIRS):
-        dk_ref[2, p] = states[p]
-    drafted(0, [dk_ref[2, p] for p in range(PAIRS)])
+        end = jnp.where(core == p // SPLIT, st_ref[p % SPLIT], endm_ref[p % SPLIT])
+        accept(0, p, jnp.where(long_own, end, halves(st0_ref[p].astype(F32))))
+    rbuf[...] = wide_ref[...].astype(BF16).reshape(64, 16, 128)
+    rgot[g] = rbuf[g]
+    scatter_rep(rbuf, rgot, b_send, b_recv, g, t)
+    for s in range(2):
+        draft_ref[DRAFT * s : DRAFT * s + DRAFT, :] = normed(
+            dy_ref[s], heads_sum, scale, shift, DRAFT, PAIRS
+        ).astype(BF16)
 
     def finish(i, _):
         rows = pl.ds(pl.multiple_of(i * CHUNK, 16), CHUNK)
@@ -523,21 +553,19 @@
     prior_ref[...] = tn(edges.astype(BF16), dealt)[0:16].astype(BF16)
     to_mate(13).wait_recv()
     tail_ref[:, mate_cols] = jnp.where(long_own, om_ref[...], jnp.zeros((TAIL, SIDE), BF16))
-    for s in range(2):
-        wait_rep(rgot.at[s], b_recv.at[s])
+    wait_rep(rgot, b_recv)
     wide_ref[...] = rgot[...].reshape(1024, 128).astype(F32)
     for c in range(8):
         rows = jnp.concatenate(
-            [wide_ref[pl.ds(c, 64, stride=8), :], wide_ref[pl.ds(512 + c, 64, stride=8), :]], axis=0
+            [wide_ref[pl.ds(c, 64, stride=16), :], wide_ref[pl.ds(8 + c, 64, stride=16), :]], axis=0
         )
         state_ref[pl.ds(c, 128, stride=8), :] = mm(by_req, rows.astype(BF16))
 
     wait_rep(pbuf, p_send)
     wait_rep(sbuf, st_send)
     wait_rep(ebuf, e_send)
-    for s in range(2):
-        wait_rep(rbuf.at[s], b_send.at[s])
-    for j in range(14):
+    wait_rep(rbuf, b_send)
+    for j in range(15):
         to_mate(j).wait_send()
     for item in range(8):
         move(item, t, right, right_send, left_recv).wait_send()
@@ -595,15 +623,16 @@
             vm((16, WID), BF16), vm((16, RANK), BF16), vm((16, WID), BF16), vm((16, RANK), BF16),
             vm((TP, ROWS, WID), BF16), vm((TP, ROWS, RANK), BF16), vm((ROWS, WID), F32),
             vm((HALF, WID), BF16), vm((HALF, RANK), BF16), vm((LATE, WID), BF16), vm((LATE, RANK), BF16),
-            vm((8, WID), F32), side, vm((TAIL, RANK), BF16), side, side,
+            side, vm((TAIL, RANK), BF16), side, side,
             vm((PAIRS, 64, 128), BF16), vm((SPLIT, 64, 128), BF16),
             vm((STEPS * SPLIT, 2 * CHUNK, CHUNK), BF16), side, vm((TAIL, SIDE), F32),
             vm((STEPS * SPLIT, 128, CHUNK), BF16), vm((STEPS * SPLIT, 128, 128), F32),
             vm((SPLIT, 128, 128), F32), vm((SPLIT, 128, 128), F32), vm((TAIL, SIDE), F32), side, side,
             vm((2, 128, 128), F32), drafts, vm((2, PAIRS, 128, 128), F32), vm((3, PAIRS, 128, 128), F32),
-            vm((2, REP, 8, 128), BF16), vm((2, REP, 8, 128), BF16), tile8, tile8,
-            DMA((19,)), DMA((TP,)), DMA, DMA, DMA, DMA, DMA, DMA, DMA((2,)), DMA((2,)), DMA((14,)), DMA((14,)),
+            tile16, tile16, tile8, tile8, vm((16, RANK), BF16),
+            DMA((19,)), DMA((TP,)), DMA, DMA, DMA, DMA, DMA, DMA, DMA, DMA, DMA((15,)), DMA((15,)),
             DMA((8,)), DMA((8,)), DMA((8,)), DMA((8,)), DMA((8,)), DMA((8,)),
+            pltpu.SemaphoreType.REGULAR, pltpu.SemaphoreType.REGULAR,
         ],
         compiler_params=pltpu.CompilerParams(
             collective_id=0, has_side_effects=True, vmem_limit_bytes=56 << 20

time: 63.9 us -> 57.8 us (0.905)
  Pallas kernels: 63.1 us -> 57.1 us
    pallas_call x1, Pallas kernels: 60.7 us -> 54.6 us  [local(): pl.pallas_call(mix_kernel, name='time_mix', out_shape=shapes, in_specs=[A...]
where the time goes in v3:
time: 57.8 us; the launch traced here: 57.7 us
  Pallas kernels  57.1 us (99%)
  between operations  0.65 us (1%)
    pallas_call x1, Pallas kernels, local(): pl.pallas_call(mix_kernel, name='time_mix', out_shape=shapes, in_specs=[A...  54.6 us
    pallas_call x1, Pallas kernels, local(): pl.pallas_call(place_kernel, name='place', out_shape=shapes, in_specs=[VM...  2.43 us

profile of v3, /device:TPU:1, one launch (start us, length us, event | category | flops | bytes accessed | tf_op | source)
XLA Modules:
  0.0 57.7 jit_solution(8267054998114191570)
XLA Ops:
  0.6 54.6 %time_mix.1 = (bf16[384,1024]{1,0:T(8,128)(2,1)}, bf16[32,1024]{1,0:T(8,128)(2,1)}, f32[1024,128]{1,0:T(8,128)}, bf16[16,128]{1,0:T(8,128)(2,1)}) custom-call(bf16[384,1024]{1,0:T(8,128)(2,1)} %bitcast.25, bf16[32,1024]{1,0:T(8,128)(2,1)} %bitcast.29, f32[1024,128]{1,0:T(8,128)} %bitcast.28, bf16[16,128]{1,0:T(8,128)(2,1)} %bitcast.32, f32[1,1024]{1,0:T(1,128)} %bitcast.33, ...), custom_call_target="tpu_custom_call" | custom-call | tf_op jit(solution)/shard_map/time_mix/pallas_call | solution.py:611
  55.3 2.4 %place.1 = (bf16[384,1024]{1,0:T(8,128)(2,1)}, bf16[32,1024]{1,0:T(8,128)(2,1)}, f32[1024,128]{1,0:T(8,128)}, bf16[16,128]{1,0:T(8,128)(2,1)}) custom-call(bf16[384,1024]{1,0:T(8,128)(2,1)} %get-tuple-element.12.a_ref, bf16[32,1024]{1,0:T(8,128)(2,1)} %get-tuple-element.13.b_ref, f32[1024,128]{1,0:T(8,128)} %get-tuple-element.14.c_ref, ...), custom_call_target="tpu_custom_call" | custom-call | tf_op jit(solution)/shard_map/place/pallas_call | solution.py:657

commit v4 on v3

--- a/solution.py
+++ b/solution.py
@@ -15,7 +15,7 @@
 TAIL = 384
 HALF = 192
 LATE = 48
-ROWS = HALF + LATE
+ROWS = HALF + 32
 PIECE = 48
 CHUNK = 32
 PAIRS = 8
@@ -30,12 +30,12 @@
 
 ITEMS = (
     ("p", 0, 192),
-    ("x", 0, 48),
+    ("x", 16, 32),
     ("x", 48, 48),
     ("x", 96, 48),
     ("x", 144, 48),
-    ("x", 192, 16),
-    ("x", 208, 32),
+    ("x", 0, 16),
+    ("x", 192, 32),
     ("p", 192, 48),
 )
 RELAY_RIGHT = (1, 3, 5)
@@ -172,13 +172,14 @@
 def mix_kernel(
     x_hbm, gx_hbm, km_hbm, p0_hbm, mc_hbm, mf_hbm, own_hbm, spans_hbm, adm_hbm, gr_hbm, gk_hbm, ex_hbm,
     anchor_hbm, boost_hbm, scale_hbm, shift_hbm, w_hbm, sh_hbm, rt_hbm, kt_hbm,
-    tail_ref, draft_ref, state_ref, prior_ref,
+    tail_hbm, draft_hbm, rgot, prior_hbm, req_hbm,
     x_ref, gx_ref, km_ref, p0_ref, mc_ref, mf_ref, own_ref, spans_ref, adm_ref, gr_ref, gk_ref, ex_ref,
     anchor_ref, boost_ref, scale_ref, shift_ref, w_ref, sh_ref, rown, kown,
     perm_ref, wide_ref, sbuf, sgot, pbuf, pgot, xv_ref, part_ref, xin, pin, zsend, zpart, zin, zpin,
     xg, pg, acc, vh, lh, vl_ref, ll_ref, vt_ref, lt_ref, rmate, kmate, st0_ref, stm_ref,
     sc_ref, ri_ref, gain_ref, kd_ref, keep_ref, st_ref, endm_ref, y_ref, o_ref, om_ref,
-    dy_ref, dri_ref, du_ref, dk_ref, rbuf, rgot, ebuf, egot, lz_ref,
+    dy_ref, dri_ref, du_ref, dk_ref, rbuf, ebuf, egot, lz_ref,
+    dkd_ref, dsc_ref, tail_ref, draft_ref, prior_ref, req_ref, out_sem,
     in_sem, w_sem, st_send, st_recv, p_send, p_recv, e_send, e_recv, b_send, b_recv, mate_send, mate_recv,
     right_send, left_recv, left_send, right_recv, hop_send, hop_recv, round1, round2,
 ):
@@ -312,11 +313,10 @@
         rows = pl.ds(j * PIECE, PIECE)
         xg[t, rows, :] = jnp.where(long_own, xv_ref[pl.ds(mine + j * PIECE, PIECE), :], xin[rows, :])
         give(1 + j)
-        if j == 1:
-            pl.semaphore_wait(round1, 4)
-            pass_on(round2, g, t, (3, 4, 5))
     to_mate(5).start()
     to_mate(6).start()
+    pl.semaphore_wait(round1, 4)
+    pass_on(round2, g, t, (3, 4, 5))
 
     hand_on(0)
     far_item(0)
@@ -372,7 +372,7 @@
             acc[:, c] = acc[:, c] + out if add else out
             return 0
 
-        lax.fori_loop(0, WID // 256, tile, 0)
+        lax.fori_loop(0, WID // 256, tile, 0, unroll=2)
 
     to_mate(5).wait_recv()
     to_mate(6).wait_recv()
@@ -407,8 +407,9 @@
         to_mate(7).wait_recv()
         to_mate(8).wait_recv()
         at = HALF + 32
-        xg[t, at : at + 16, :] = jnp.where(long_own, zsend[...], zin[...])
         pg[t, at : at + 16, :] = jnp.where(long_own, zpart[...], zpin[...])
+        first_rows = jnp.where(long_own, zsend[...], zin[...])
+        xg[t, 0:16, :] = jnp.where(core == 0, first_rows, xg[t, 0:16, :])
         for item in (7, 5, 6):
             give(item)
 
@@ -427,13 +428,55 @@
         egot[g] = ebuf[g]
         scatter_rep(ebuf, egot, e_send, e_recv, g, t)
 
-    lax.fori_loop(1, 4, ready, 0)
+    def draft_ready(s):
+        rows = slice(DRAFT * s, DRAFT * s + DRAFT)
+        log = -jnp.exp(anchor + mm(ll_ref[rows, :], ex_ref[...]))
+        r, k = gr_ref[rows, :].astype(F32), gk_ref[rows, :].astype(F32)
+        incl = running(log, DRAFT)
+        q, kk, ri = scaled(r, k, incl, log, DRAFT)
+        dri_ref[rows, :] = ri
+        gain = mm(stack((r * boost * k).astype(BF16), PAIRS), heads_sum)
+        taken = row16 < counts[s]
+        upto = jnp.sum(jnp.where(taken, log, 0.0), axis=0, keepdims=True)
+        weight = jnp.where(taken, jnp.exp(jnp.where(taken, upto - incl, 0.0)), 0.0)
+        dkd_ref[rows, :] = (k * weight).astype(BF16)
+        keep = jnp.exp(upto)
+        dy_ref[s] = gain
+        for p in range(PAIRS):
+            c = lanes(p)
+            dsc_ref[PAIRS * s + p] = scored(q[:, c], kk[:, c], DRAFT)
+            dk_ref[s, p] = column(keep[:, c])
+
+    def draft_values(s):
+        rows = slice(DRAFT * s, DRAFT * s + DRAFT)
+        low16 = iota((DRAFT, 128), 1) < SPAN
+        for p in range(PAIRS):
+            c = lanes(p)
+            at = slice(DRAFT * p, DRAFT * p + DRAFT)
+            v = vl_ref[rows, c]
+            both = mm(dsc_ref[PAIRS * s + p], v)
+            inner = jnp.where(low16, both[0:DRAFT], both[DRAFT : 2 * DRAFT])
+            dy_ref[s, at, :] = inner + dy_ref[s, at, :] * v.astype(F32)
+            du_ref[s, p] = jnp.where(same, tn(dkd_ref[rows, c], v), 0.0)
+
+    lax.fori_loop(1, 4, ready, 0, unroll=3)
     hand_on(3)
     late_rows()
+    lax.fori_loop(4, 6, ready, 0, unroll=2)
+    give_late()
     hand_on(4)
-    lax.fori_loop(4, 6, ready, 0)
-    give_late()
+    lax.fori_loop(6, 9, ready, 0, unroll=3)
     edges_out()
+    for k in range(TP):
+        w_copy(k).wait()
+    product(t, False)
+    hand_on(7)
+    hand_on(5)
+    hand_on(6)
+    far_item(7)
+    ll_ref[...] = low_rank(HALF, LATE)
+    to_mate(14).start()
+    product(left, True)
     wait_rep(sgot, st_recv)
     wide_ref[...] = sgot[...].reshape(1024, 128).astype(F32)
     for p in range(PAIRS):
@@ -441,17 +484,7 @@
     to_mate(11).start()
     for p in range(PAIRS):
         dk_ref[2, p] = halves(wide_ref[pl.ds(8 + p, 64, stride=16), :])
-    lax.fori_loop(6, STEPS, ready, 0)
-    for k in range(TP):
-        w_copy(k).wait()
-    hand_on(7)
-    far_item(7)
-    hand_on(5)
-    hand_on(6)
-    ll_ref[...] = low_rank(HALF, LATE)
-    to_mate(14).start()
-    product(t, False)
-    product(left, True)
+    lax.fori_loop(9, STEPS, ready, 0, unroll=3)
     to_mate(14).wait_recv()
     head = jnp.where(core == 0, ll_ref[32:33, :], lz_ref[0:1, :])
     lt_ref[0:16, :] = jnp.where(iota((16, RANK), 0) == 0, head, lt_ref[0:16, :])
@@ -461,48 +494,32 @@
     for p in range(SPLIT):
         start = jnp.where(long_own, st0_ref[core * SPLIT + p], stm_ref[p])
         st_ref[p] = halves(start.astype(F32))
+    for s in range(2):
+        draft_ready(s)
     for item in range(1, 7):
         far_item(item)
     product(far, True)
     vh[...] = acc[0:HALF, :].astype(BF16)
+    to_mate(10).start()
     vl_ref[...] = acc[HALF:ROWS, :].astype(BF16)
-    vh[0:16, :] = jnp.where((row16 == 0) & (core == 0), vl_ref[32:33, :], vh[0:16, :])
-    to_mate(10).start()
     vt_ref[pl.ds(mine, HALF), :] = vh[:, cols]
-
-    low16 = iota((DRAFT, 128), 1) < SPAN
-
-    def draft_ready(s):
-        rows = slice(DRAFT * s, DRAFT * s + DRAFT)
-        log = -jnp.exp(anchor + mm(ll_ref[rows, :], ex_ref[...]))
-        r, k, v = gr_ref[rows, :].astype(F32), gk_ref[rows, :].astype(F32), vl_ref[rows, :]
-        incl = running(log, DRAFT)
-        q, kk, ri = scaled(r, k, incl, log, DRAFT)
-        dri_ref[rows, :] = ri
-        gain = mm(stack((r * boost * k).astype(BF16), PAIRS), heads_sum)
-        taken = row16 < counts[s]
-        upto = jnp.sum(jnp.where(taken, log, 0.0), axis=0, keepdims=True)
-        weight = jnp.where(taken, jnp.exp(jnp.where(taken, upto - incl, 0.0)), 0.0)
-        kd = (k * weight).astype(BF16)
-        keep = jnp.exp(upto)
-        for p in range(PAIRS):
-            c = lanes(p)
-            both = mm(scored(q[:, c], kk[:, c], DRAFT), v[:, c])
-            inner = jnp.where(low16, both[0:DRAFT], both[DRAFT : 2 * DRAFT])
-            dy_ref[s, DRAFT * p : DRAFT * p + DRAFT, :] = (
-                inner + gain[DRAFT * p : DRAFT * p + DRAFT] * v[:, c].astype(F32)
-            )
-            du_ref[s, p] = jnp.where(same, tn(kd[:, c], v[:, c]), 0.0)
-            dk_ref[s, p] = column(keep[:, c])
 
     def accept(s, p, state):
         rows = slice(DRAFT * s, DRAFT * s + DRAFT)
         at = slice(DRAFT * p, DRAFT * p + DRAFT)
         dy_ref[s, at, :] = dy_ref[s, at, :] + mm(dri_ref[rows, lanes(p)], state.astype(BF16))
         end = state * dk_ref[s, p] + du_ref[s, p]
-        wide_ref[pl.ds(8 * s + p, 64, stride=16), :] = end[0:64] + end[64:128]
-
-    draft_ready(0)
+        wide_ref[pl.ds(512 * s + p, 64, stride=8), :] = end[0:64] + end[64:128]
+
+    def give_back(s):
+        rbuf[s] = wide_ref[512 * s : 512 * s + 512, :].astype(BF16).reshape(64, 8, 128)
+        rgot[s, g] = rbuf[s, g]
+        scatter_rep(rbuf.at[s], rgot.at[s], b_send.at[s], b_recv.at[s], g, t)
+
+    draft_values(1)
+    for p in range(PAIRS):
+        accept(1, p, dk_ref[2, p])
+    give_back(1)
 
     to_mate(10).wait_recv()
     low32 = iota((CHUNK, 128), 1) < SPAN
@@ -519,23 +536,10 @@
             st_ref[p] = state * keep_ref[SPLIT * i + p] + jnp.where(same, mm(kd_ref[SPLIT * i + p], v), 0.0)
         return 0
 
-    lax.fori_loop(0, STEPS, step, 0, unroll=3)
+    lax.fori_loop(0, STEPS, step, 0, unroll=6)
     to_mate(12).start()
 
-    draft_ready(1)
-    for p in range(PAIRS):
-        accept(1, p, dk_ref[2, p])
-    to_mate(12).wait_recv()
-    for p in range(PAIRS):
-        end = jnp.where(core == p // SPLIT, st_ref[p % SPLIT], endm_ref[p % SPLIT])
-        accept(0, p, jnp.where(long_own, end, halves(st0_ref[p].astype(F32))))
-    rbuf[...] = wide_ref[...].astype(BF16).reshape(64, 16, 128)
-    rgot[g] = rbuf[g]
-    scatter_rep(rbuf, rgot, b_send, b_recv, g, t)
-    for s in range(2):
-        draft_ref[DRAFT * s : DRAFT * s + DRAFT, :] = normed(
-            dy_ref[s], heads_sum, scale, shift, DRAFT, PAIRS
-        ).astype(BF16)
+    draft_values(0)
 
     def finish(i, _):
         rows = pl.ds(pl.multiple_of(i * CHUNK, 16), CHUNK)
@@ -543,8 +547,18 @@
         o_ref[rows, :] = normed(y, heads_sum, scale_ref[:, cols], shift_ref[:, cols], CHUNK, SPLIT).astype(BF16)
         return 0
 
-    lax.fori_loop(0, STEPS, finish, 0)
+    lax.fori_loop(0, STEPS // 2, finish, 0, unroll=2)
+    to_mate(12).wait_recv()
+    for p in range(PAIRS):
+        end = jnp.where(core == p // SPLIT, st_ref[p % SPLIT], endm_ref[p % SPLIT])
+        accept(0, p, jnp.where(long_own, end, halves(st0_ref[p].astype(F32))))
+    give_back(0)
+    lax.fori_loop(STEPS // 2, STEPS, finish, 0, unroll=2)
     to_mate(13).start()
+    for s in range(2):
+        draft_ref[DRAFT * s : DRAFT * s + DRAFT, :] = normed(
+            dy_ref[s], heads_sum, scale, shift, DRAFT, PAIRS
+        ).astype(BF16)
     tail_ref[:, cols] = jnp.where(long_own, o_ref[...], jnp.zeros((TAIL, SIDE), BF16))
 
     wait_rep(egot, e_recv)
@@ -553,18 +567,21 @@
     prior_ref[...] = tn(edges.astype(BF16), dealt)[0:16].astype(BF16)
     to_mate(13).wait_recv()
     tail_ref[:, mate_cols] = jnp.where(long_own, om_ref[...], jnp.zeros((TAIL, SIDE), BF16))
-    wait_rep(rgot, b_recv)
-    wide_ref[...] = rgot[...].reshape(1024, 128).astype(F32)
-    for c in range(8):
-        rows = jnp.concatenate(
-            [wide_ref[pl.ds(c, 64, stride=16), :], wide_ref[pl.ds(8 + c, 64, stride=16), :]], axis=0
-        )
-        state_ref[pl.ds(c, 128, stride=8), :] = mm(by_req, rows.astype(BF16))
+    req_ref[...] = by_req
+    outs = ((tail_ref, tail_hbm), (draft_ref, draft_hbm), (prior_ref, prior_hbm), (req_ref, req_hbm))
+    puts = [pltpu.make_async_copy(a, b, out_sem.at[i]) for i, (a, b) in enumerate(outs)]
+    for put in puts:
+        put.start()
+    for s in range(2):
+        wait_rep(rgot.at[s], b_recv.at[s])
+    for put in puts:
+        put.wait()
 
     wait_rep(pbuf, p_send)
     wait_rep(sbuf, st_send)
     wait_rep(ebuf, e_send)
-    wait_rep(rbuf, b_send)
+    for s in range(2):
+        wait_rep(rbuf.at[s], b_send.at[s])
     for j in range(15):
         to_mate(j).wait_send()
     for item in range(8):
@@ -573,13 +590,30 @@
         move(item, far, right, hop_send, hop_recv).wait_send()
 
 
-def place_kernel(a_ref, b_ref, c_ref, d_ref, a_out, b_out, c_out, d_out, sem):
-    pairs = ((a_ref, a_out), (b_ref, b_out), (c_ref, c_out), (d_ref, d_out))
-    copies = [pltpu.make_async_copy(src, dst, sem.at[i]) for i, (src, dst) in enumerate(pairs)]
-    for c in copies:
-        c.start()
-    for c in copies:
-        c.wait()
+def place_kernel(
+    tail_in, draft_in, back_in, prior_in, req_in, tail_out, draft_out, state_out, prior_out,
+    tail, draft, back, prior, req, wide, state, get_sem, put_sem,
+):
+    src, mid = (back_in, req_in, tail_in, draft_in, prior_in), (back, req, tail, draft, prior)
+    gets = [pltpu.make_async_copy(a, b, get_sem.at[i]) for i, (a, b) in enumerate(zip(src, mid))]
+    outs = ((tail, tail_out), (draft, draft_out), (prior, prior_out), (state, state_out))
+    puts = [pltpu.make_async_copy(a, b, put_sem.at[i]) for i, (a, b) in enumerate(outs)]
+    for get in gets:
+        get.start()
+    gets[0].wait()
+    gets[1].wait()
+    wide[...] = back[...].reshape(1024, 128).astype(F32)
+    for i in range(3):
+        gets[2 + i].wait()
+        puts[i].start()
+    for c in range(8):
+        rows = jnp.concatenate(
+            [wide[pl.ds(c, 64, stride=8), :], wide[pl.ds(512 + c, 64, stride=8), :]], axis=0
+        )
+        state[pl.ds(c, 128, stride=8), :] = mm(req[...], rows.astype(BF16))
+    puts[3].start()
+    for put in puts:
+        put.wait()
 
 
 VM = pl.BlockSpec(memory_space=pltpu.VMEM)
@@ -611,9 +645,9 @@
     outs = pl.pallas_call(
         mix_kernel,
         name="time_mix",
-        out_shape=shapes,
+        out_shape=(shapes[0], shapes[1], sds((2, REP, 8, 128), BF16), shapes[3], sds((128, 128), BF16)),
         in_specs=[ANY] * 20,
-        out_specs=(VM,) * 4,
+        out_specs=(ANY, ANY, VM, ANY, ANY),
         scratch_shapes=[
             vm((TAIL, WID), BF16), drafts, vm((1024, 128), F32), vm((16, 128), BF16), row, row,
             ints, ints, ints, drafts, drafts, vm((RANK, WID), BF16), row, row, row, row,
@@ -621,16 +655,18 @@
             vm((128, 128), F32), vm((1024, 128), F32), tile16, tile16, tile8, tile8,
             vm((TAIL, WID), BF16), vm((TAIL, RANK), BF16), vm((HALF, WID), BF16), vm((HALF, RANK), BF16),
             vm((16, WID), BF16), vm((16, RANK), BF16), vm((16, WID), BF16), vm((16, RANK), BF16),
-            vm((TP, ROWS, WID), BF16), vm((TP, ROWS, RANK), BF16), vm((ROWS, WID), F32),
-            vm((HALF, WID), BF16), vm((HALF, RANK), BF16), vm((LATE, WID), BF16), vm((LATE, RANK), BF16),
+            vm((TP, ROWS, WID), BF16), vm((TP, HALF + LATE, RANK), BF16), vm((ROWS, WID), F32),
+            vm((HALF, WID), BF16), vm((HALF, RANK), BF16), vm((32, WID), BF16), vm((LATE, RANK), BF16),
             side, vm((TAIL, RANK), BF16), side, side,
             vm((PAIRS, 64, 128), BF16), vm((SPLIT, 64, 128), BF16),
             vm((STEPS * SPLIT, 2 * CHUNK, CHUNK), BF16), side, vm((TAIL, SIDE), F32),
             vm((STEPS * SPLIT, 128, CHUNK), BF16), vm((STEPS * SPLIT, 128, 128), F32),
             vm((SPLIT, 128, 128), F32), vm((SPLIT, 128, 128), F32), vm((TAIL, SIDE), F32), side, side,
             vm((2, 128, 128), F32), drafts, vm((2, PAIRS, 128, 128), F32), vm((3, PAIRS, 128, 128), F32),
-            tile16, tile16, tile8, tile8, vm((16, RANK), BF16),
-            DMA((19,)), DMA((TP,)), DMA, DMA, DMA, DMA, DMA, DMA, DMA, DMA, DMA((15,)), DMA((15,)),
+            vm((2, REP, 8, 128), BF16), tile8, tile8, vm((16, RANK), BF16),
+            drafts, vm((2 * PAIRS, 2 * DRAFT, DRAFT), BF16), vm((TAIL, WID), BF16), drafts, vm((16, 128), BF16),
+            vm((128, 128), BF16), DMA((4,)),
+            DMA((19,)), DMA((TP,)), DMA, DMA, DMA, DMA, DMA, DMA, DMA((2,)), DMA((2,)), DMA((15,)), DMA((15,)),
             DMA((8,)), DMA((8,)), DMA((8,)), DMA((8,)), DMA((8,)), DMA((8,)),
             pltpu.SemaphoreType.REGULAR, pltpu.SemaphoreType.REGULAR,
         ],
@@ -658,9 +694,12 @@
         place_kernel,
         name="place",
         out_shape=shapes,
-        in_specs=[VM] * 4,
+        in_specs=[ANY] * 5,
         out_specs=(ANY,) * 4,
-        scratch_shapes=[DMA((4,))],
+        scratch_shapes=[
+            vm((TAIL, WID), BF16), drafts, vm((2, REP, 8, 128), BF16), vm((16, 128), BF16),
+            vm((128, 128), BF16), vm((1024, 128), F32), vm((1024, 128), F32), DMA((5,)), DMA((4,)),
+        ],
     )(*outs)
     return (
         tail.reshape(1, TAIL, WID),

time: 57.8 us -> 54 us (0.934)
  Pallas kernels: 57.1 us -> 53.3 us
    pallas_call x2, Pallas kernels: 57.1 us -> 53.3 us  [the longest x1 50.9 us: local(): pl.pallas_call(mix_kernel, name='time_mix', out_shape=(shapes[0], shapes[...]
where the time goes in v4:
time: 54 us; the launch traced here: 53.9 us
  Pallas kernels  53.3 us (99%)
  between operations  0.65 us (1%)
    pallas_call x1, Pallas kernels, local(): pl.pallas_call(mix_kernel, name='time_mix', out_shape=(shapes[0], shapes[...  50.9 us
    pallas_call x1, Pallas kernels, local(): pl.pallas_call(place_kernel, name='place', out_shape=shapes, in_specs=[AN...  2.39 us

profile of v4, /device:TPU:1, one launch (start us, length us, event | category | flops | bytes accessed | tf_op | source)
XLA Modules:
  0.0 53.9 jit_solution(15938439247276869777)
XLA Ops:
  0.6 50.9 %time_mix.1 = (bf16[384,1024]{1,0:T(8,128)(2,1)}, bf16[32,1024]{1,0:T(8,128)(2,1)}, bf16[2,64,8,128]{3,2,1,0:T(8,128)(2,1)}, bf16[16,128]{1,0:T(8,128)(2,1)}, bf16[128,128]{1,0:T(8,128)(2,1)}) custom-call(bf16[384,1024]{1,0:T(8,128)(2,1)} %bitcast.25, bf16[32,1024]{1,0:T(8,128)(2,1)} %bitcast.29, f32[1024,128]{1,0:T(8,128)} %bitcast.28, ...), custom_call_target="tpu_custom_call" | custom-call | tf_op jit(solution)/shard_map/time_mix/pallas_call | solution.py:645
  51.5 2.4 %place.1 = (bf16[384,1024]{1,0:T(8,128)(2,1)}, bf16[32,1024]{1,0:T(8,128)(2,1)}, f32[1024,128]{1,0:T(8,128)}, bf16[16,128]{1,0:T(8,128)(2,1)}) custom-call(bf16[384,1024]{1,0:T(8,128)(2,1)} %get-tuple-element.13.tail_in, bf16[32,1024]{1,0:T(8,128)(2,1)} %get-tuple-element.14.draft_in, bf16[2,64,8,128]{3,2,1,0:T(8,128)(2,1)} %get-tuple-element.15.back_in, ...), custom_call_target="tpu_custom_call" | custom-call | tf_op jit(solution)/shard_map/place/pallas_call | solution.py:693

commit v5 on v4

--- a/solution.py
+++ b/solution.py
@@ -372,7 +372,7 @@
             acc[:, c] = acc[:, c] + out if add else out
             return 0
 
-        lax.fori_loop(0, WID // 256, tile, 0, unroll=2)
+        lax.fori_loop(0, WID // 256, tile, 0, unroll=4)
 
     to_mate(5).wait_recv()
     to_mate(6).wait_recv()

time: 54 us -> 52.8 us (0.978)
  Pallas kernels: 53.3 us -> 52.1 us
    pallas_call x1, Pallas kernels: 50.9 us -> 49.7 us  [local(): pl.pallas_call(mix_kernel, name='time_mix', out_shape=(shapes[0], shapes[...]
where the time goes in v5:
time: 52.8 us; the launch traced here: 52.7 us
  Pallas kernels  52.1 us (99%)
  between operations  0.65 us (1%)
    pallas_call x1, Pallas kernels, local(): pl.pallas_call(mix_kernel, name='time_mix', out_shape=(shapes[0], shapes[...  49.7 us
    pallas_call x1, Pallas kernels, local(): pl.pallas_call(place_kernel, name='place', out_shape=shapes, in_specs=[AN...  2.39 us

profile of v5, /device:TPU:1, one launch (start us, length us, event | category | flops | bytes accessed | tf_op | source)
XLA Modules:
  0.0 52.7 jit_solution(1481286001731211428)
XLA Ops:
  0.6 49.7 %time_mix.1 = (bf16[384,1024]{1,0:T(8,128)(2,1)}, bf16[32,1024]{1,0:T(8,128)(2,1)}, bf16[2,64,8,128]{3,2,1,0:T(8,128)(2,1)}, bf16[16,128]{1,0:T(8,128)(2,1)}, bf16[128,128]{1,0:T(8,128)(2,1)}) custom-call(bf16[384,1024]{1,0:T(8,128)(2,1)} %bitcast.25, bf16[32,1024]{1,0:T(8,128)(2,1)} %bitcast.29, f32[1024,128]{1,0:T(8,128)} %bitcast.28, ...), custom_call_target="tpu_custom_call" | custom-call | tf_op jit(solution)/shard_map/time_mix/pallas_call | solution.py:645
  50.3 2.4 %place.1 = (bf16[384,1024]{1,0:T(8,128)(2,1)}, bf16[32,1024]{1,0:T(8,128)(2,1)}, f32[1024,128]{1,0:T(8,128)}, bf16[16,128]{1,0:T(8,128)(2,1)}) custom-call(bf16[384,1024]{1,0:T(8,128)(2,1)} %get-tuple-element.13.tail_in, bf16[32,1024]{1,0:T(8,128)(2,1)} %get-tuple-element.14.draft_in, bf16[2,64,8,128]{3,2,1,0:T(8,128)(2,1)} %get-tuple-element.15.back_in, ...), custom_call_target="tpu_custom_call" | custom-call | tf_op jit(solution)/shard_map/place/pallas_call | solution.py:693
